TPU v7x, 128 devices: a whole 4x4x4 slice. The times are simulated.
128 devices in a mesh: zone: 32 (over y, x, core), sub: 4 (over z).
Axes of the slice: x: 4, y: 4, z: 4, core: 2. Of those that a mesh axis runs over, the one named last changes fastest.
Arguments:
- order_features: bfloat16 [262144, 128], P('zone'), may hold values from -6 to 6
- w_in: bfloat16 [128, 512], replicated, may hold values from -0.5 to 0.5
- bias_in: float32 [512], replicated, may hold values from -3 to 3
- w_out: bfloat16 [512, 128], replicated, may hold values from -0.25 to 0.25
- bias_out: float32 [128], replicated, may hold values from -3 to 3
- courier_embed: bfloat16 [65536, 128], P(('zone', 'sub')), may hold values from -28 to 28
- courier_cap: bfloat16 [65536], P(('zone', 'sub')), may hold values from 0.5 to 4
- adjacency: int32 [512, 8], P('zone'), may hold values from 0 to 127, all different within a row; in each aligned block of 16 rows (0 to 15, 16 to 31, ...) at most 2 rows name the same one
- order_count: int32 [512], P('zone'), may hold values from 64 to 512
- courier_count: int32 [128], P(('zone', 'sub')), may hold values from 64 to 512
Outputs:
- order_potentials: float32 [262144], P('zone')
- courier_potentials: float32 [65536], P(('zone', 'sub'))
Inputs may be any that keep to these rules, and one draw needn't show every extreme that they name: `adjacency`: each row names 8 different courier blocks and every courier block is named by some row. Among the 16 rows of one index of zone (aligned blocks of rows), no courier block is named by more than 2 rows, and in some of them one is named by exactly 2.
All inputs are finite; a program needn't handle non-finite values.
Results may differ from a plain program's by a relative error of at most 0.0017.
Values may be sent and summed in bfloat16 or wider, within the bound.
No kernel may reach another device: no remote copies, remote signals or barrier semaphores. Data moves between devices by JAX's collectives and lax.ppermute only.
A program may use at most 128 MiB of HBM per device.

v0:
```python
import math

import jax
import jax.numpy as jnp
from jax import lax
from jax.experimental import pallas as pl
from jax.experimental.pallas import tpu as pltpu
from jax.sharding import PartitionSpec as P

BLOCK = 512
EMB = 128
HID = 512
ADJ = 8
OB_DEV = 16
ZONES = 32
SUBS = 4
HALF = 256
COURIER_ROWS = BLOCK + 16
UNROLL = 32
REST = 8
MOST_ENTRIES = 256
LIST_SIZE = MOST_ENTRIES + 2 * REST
NO_ORDER = 2 * OB_DEV
NO_COURIER = 2 * ZONES

TEMPER = 0.2
LOWEST = -1e30
SCORE_SCALE = math.log2(math.e) / (TEMPER * math.sqrt(EMB))
DUAL_SCALE = TEMPER * math.log(2.0)

VMEM_LIMIT = 16 * 1024 * 1024
PARTS = 8


def zone_of(y, x, core):
    return ((y % 4) * 4 + (x % 4)) * 2 + core


PLACES = [(y, x, core) for y in range(4) for x in range(4) for core in range(2)]


def other_core(value):
    return lax.ppermute(value, "zone", [(zone_of(y, x, c), zone_of(y, x, 1 - c)) for y, x, c in PLACES])


def along_z(value, step):
    return lax.ppermute(value, "sub", [(i, (i + step) % SUBS) for i in range(SUBS)])


def plane_step(value, stage, step):
    pairs = []
    for y, x, c in PLACES:
        to = (y, x + step, c) if stage == c else (y + step, x, c)
        pairs.append((zone_of(y, x, c), zone_of(*to)))
    return lax.ppermute(value, "zone", pairs)


def gather_row(block):
    return jnp.concatenate([block] + [plane_step(block, 0, step) for step in (1, 2, 3)], axis=0)


def gather_plane(row, meanwhile):
    own = [row] + [plane_step(row, 1, step) for step in (1, 2, 3)]
    swapped = [other_core(row)]
    own[1], own[2], own[3], meanwhile = lax.optimization_barrier((own[1], own[2], own[3], meanwhile))
    return own + swapped + [other_core(part) for part in own[1:]], meanwhile


def slot_of(zone, me):
    back_x = ((me >> 1) - (zone >> 1)) & 3
    back_y = ((me >> 3) - (zone >> 3)) & 3
    odd = zone & 1
    first = jnp.where(odd == 0, back_x, back_y)
    second = jnp.where(odd == 0, back_y, back_x)
    return ((me ^ zone) & 1) * 16 + second * 4 + first


def join(*parts):
    highest = parts[0]
    for part in parts[1:]:
        highest = jnp.maximum(highest, part)
    total = jnp.exp2(parts[0] - highest)
    for part in parts[1:]:
        total = total + jnp.exp2(part - highest)
    return highest + jnp.log2(total)


def join_subs(value):
    return join(value, along_z(value, 1), along_z(value, 2), along_z(value, 3))


def join_zones(value):
    value = join(value, other_core(value))
    for stage in range(2):
        value = join(value, *[plane_step(value, stage, step) for step in (1, 2, 3)])
    return value


EMBED_ROWS = 4096


def embed_kernel(x_hbm, w_in_hbm, b_in_hbm, w_out_hbm, b_out_hbm, o_ref, x_ref, w_in_ref, b_in_ref, w_out_ref, b_out_ref, sem):
    steps = x_ref.shape[0] // EMBED_ROWS

    def rows_copy(i):
        rows = pl.ds(pl.multiple_of(i * EMBED_ROWS, EMBED_ROWS), EMBED_ROWS)
        return pltpu.make_async_copy(x_hbm.at[rows, :], x_ref.at[rows, :], sem.at[i])

    parameters = [
        pltpu.make_async_copy(source, target, sem.at[steps + i])
        for i, (source, target) in enumerate(
            [(w_in_hbm, w_in_ref), (b_in_hbm, b_in_ref), (w_out_hbm, w_out_ref), (b_out_hbm, b_out_ref)]
        )
    ]
    for copy in parameters:
        copy.start()
    for i in range(steps):
        rows_copy(i).start()
    for copy in parameters:
        copy.wait()

    def one_step(i, carry):
        rows_copy(i).wait()
        for start in range(0, EMBED_ROWS, BLOCK):
            rows = pl.ds(pl.multiple_of(i * EMBED_ROWS + start, BLOCK), BLOCK)
            v = jnp.dot(x_ref[rows, :], w_in_ref[...], preferred_element_type=jnp.float32)
            v = 0.5 * (v + b_in_ref[...])
            hidden = (v + v * jnp.tanh(v)).astype(jnp.bfloat16)
            out = jnp.dot(hidden, w_out_ref[...], preferred_element_type=jnp.float32)
            o_ref[rows, :] = ((out + b_out_ref[...]) * SCORE_SCALE).astype(jnp.bfloat16)
        return carry

    lax.fori_loop(0, steps, one_step, 0)


def embed_orders(features, w_in, bias_in, w_out, bias_out):
    rows = features.shape[0]
    operands = (features, w_in, bias_in.reshape(1, HID), w_out, bias_out.reshape(1, EMB))
    return pl.pallas_call(
        embed_kernel,
        out_shape=jax.ShapeDtypeStruct((rows, EMB), jnp.bfloat16),
        in_specs=[pl.BlockSpec(memory_space=pltpu.HBM)] * len(operands),
        out_specs=pl.BlockSpec(memory_space=pltpu.VMEM),
        scratch_shapes=[pltpu.VMEM(value.shape, value.dtype) for value in operands]
        + [pltpu.SemaphoreType.DMA((rows // EMBED_ROWS + 4,))],
        compiler_params=pltpu.CompilerParams(vmem_limit_bytes=VMEM_LIMIT),
        cost_estimate=pl.CostEstimate(
            flops=4 * rows * EMB * HID, bytes_accessed=4 * rows * EMB, transcendentals=rows * HID
        ),
        name="embed_orders",
    )(*[pltpu.with_memory_space_constraint(value, pltpu.HBM) for value in operands])


def list_kernel(pair_ref, two_ref, list_ref, rounds_ref):
    def one_pair(p, n):
        e = pair_ref[p]
        mine = (e >> 24) & 1
        order_two = (e >> 25) & 1
        courier_two = mine * two_ref[(e >> 9) & 31]
        e = e & 0xFFFFFF
        list_ref[n] = e
        n = n + mine
        list_ref[n] = e + 257
        n = n + courier_two
        list_ref[n] = e + 65536
        n = n + order_two
        list_ref[n] = e + 65536 + 257
        return n + (order_two & courier_two)

    n = lax.fori_loop(0, OB_DEV * ADJ, one_pair, jnp.int32(0), unroll=8)
    for i in range(REST):
        list_ref[n + i] = jnp.int32(NO_ORDER * 65536 + NO_COURIER * 256)
    rounds_ref[0] = (n + REST - 1) // REST


def work_list(adjacency, order_count, courier_two, name):
    zone, sub = lax.axis_index("zone"), lax.axis_index("sub")
    flat = adjacency.reshape(-1)
    z = flat >> 2
    mine = jnp.where((flat & 3) == sub, 1, 0)
    two = jnp.repeat(jnp.where(order_count > HALF, 1, 0), ADJ)
    block = jnp.arange(OB_DEV * ADJ, dtype=jnp.int32) // ADJ
    entry = (2 * block << 16) + (2 * z << 8) + 2 * slot_of(z, zone)
    pairs = entry + (mine << 24) + ((mine * two) << 25)
    smem = pl.BlockSpec(memory_space=pltpu.SMEM)
    return pl.pallas_call(
        list_kernel,
        out_shape=(
            jax.ShapeDtypeStruct((LIST_SIZE,), jnp.int32),
            jax.ShapeDtypeStruct((1,), jnp.int32),
        ),
        in_specs=[smem] * 2,
        out_specs=(smem, smem),
        compiler_params=pltpu.CompilerParams(vmem_limit_bytes=1024 * 1024),
        name=name,
    )(pairs.astype(jnp.int32), courier_two)


def pass_kernel(sum_couriers, list_ref, rounds_ref, summed_ref, kept_ref, weight_ref, live_ref, out_ref, w_ref, r_ref, m_ref):
    summed_blocks, kept_blocks = weight_ref.shape[0], live_ref.shape[0]
    rounds = rounds_ref[0]
    weight = weight_ref[...]

    high = weight.astype(jnp.bfloat16).astype(jnp.float32)
    low = weight - high
    blank = jnp.zeros((64 - 2 * summed_blocks, 128), jnp.float32)
    for part in range(2):
        rows = []
        for value in (high, low):
            rows += [value[:, part * 128 : part * 128 + 128], value[:, HALF + part * 128 : HALF + part * 128 + 128]]
            if summed_blocks < 32:
                rows.append(blank)
        w_ref[part * 128 : part * 128 + 128, :] = jnp.transpose(jnp.concatenate(rows, axis=0)).astype(jnp.bfloat16)
    r_ref[...] = jnp.zeros(r_ref.shape, jnp.float32)
    lanes = lax.broadcasted_iota(jnp.int32, (1, 128), 1) % 64

    def piece(e):
        order, courier, slot = e >> 16, (e >> 8) & 255, e & 255
        order_row = jnp.minimum(order, 2 * OB_DEV - 1) * HALF
        courier_row = (slot >> 1) * COURIER_ROWS + (slot & 1) * HALF
        return (courier, order, courier_row, order_row) if sum_couriers else (order, courier, order_row, courier_row)

    def sides(s_row, k_row):
        left = summed_ref[pl.ds(pl.multiple_of(s_row, 16), HALF), :]
        right = kept_ref[pl.ds(pl.multiple_of(k_row, 16), HALF), :]
        return left, right

    def scores(left, right):
        return lax.dot_general(left, right, (((1,), (1,)), ((), ())), preferred_element_type=jnp.float32)

    def weighted(s, s_row, k_row):
        left, right = sides(s_row, k_row)
        lane = (s % 2) * summed_blocks + s // 2
        ones = jnp.where(lanes == lane, 1.0, 0.0).astype(jnp.bfloat16)
        left = jnp.concatenate([left, w_ref[...]], axis=1)
        right = jnp.concatenate([right, jnp.broadcast_to(ones, (HALF, 128))], axis=1)
        return scores(left, right)

    def steps(first, count):
        todo = [piece(list_ref[first + t]) for t in range(count)]
        sums = [
            jnp.sum(jnp.exp2(weighted(s, s_row, k_row)).reshape(HALF // 8, 8, HALF), axis=0)
            for s, _, s_row, k_row in todo
        ]
        for (_, k, _, _), part in zip(todo, sums):
            r_ref[k // 2, k % 2] += part

    large = rounds // (UNROLL // REST)

    def large_step(i, carry):
        steps(i * UNROLL, UNROLL)
        return carry

    def small_step(i, carry):
        steps(i * REST, REST)
        return carry

    lax.fori_loop(0, large, large_step, 0)
    lax.fori_loop(large * (UNROLL // REST), rounds, small_step, 0)

    live_weight = jnp.where(weight > 0.5 * LOWEST, jnp.abs(weight), 0.0)
    bad = jnp.where(jnp.max(live_weight) <= 128.0, 0.0, 1.0)
    for half in range(2):
        cut = slice(half * HALF, (half + 1) * HALF)
        total = jnp.sum(r_ref[0:kept_blocks, half], axis=1)
        live = live_ref[:, cut] > 0.5 * LOWEST
        fine = (total >= 2.0**-86) & (total <= 2.0**126)
        bad = bad + jnp.max(jnp.where(live, jnp.where(fine, 0.0, 1.0), 0.0))
        out_ref[:, cut] = jnp.where(live, jnp.log2(jnp.where(live, total, 1.0)), LOWEST)

    @pl.when(bad > 0.0)
    def _():
        m_ref[...] = jnp.full(m_ref.shape, LOWEST, jnp.float32)
        r_ref[...] = jnp.zeros(r_ref.shape, jnp.float32)

        def one_piece(i, carry):
            s, k, s_row, k_row = piece(list_ref[i])
            block = jnp.minimum(s // 2, summed_blocks - 1)
            w = weight_ref[pl.ds(block, 1), pl.ds(pl.multiple_of((s % 2) * HALF, HALF), HALF)]
            column = jnp.transpose(jnp.broadcast_to(w, (128, HALF)))
            x = scores(*sides(s_row, k_row)) + jnp.concatenate([column, column], axis=1)
            before = m_ref[k // 2, k % 2, 0:1]
            after = jnp.maximum(before, jnp.max(x, axis=0, keepdims=True))
            scaled = r_ref[k // 2, k % 2, 0:1] * jnp.exp2(before - after)
            m_ref[k // 2, k % 2, 0:1] = after
            r_ref[k // 2, k % 2, 0:1] = scaled + jnp.sum(jnp.exp2(x - after), axis=0, keepdims=True)
            return carry

        lax.fori_loop(0, rounds * REST, one_piece, 0)
        for half in range(2):
            cut = slice(half * HALF, (half + 1) * HALF)
            live = live_ref[:, cut] > 0.5 * LOWEST
            total = jnp.where(live, r_ref[0:kept_blocks, half, 0, :], 1.0)
            out_ref[:, cut] = jnp.where(live, m_ref[0:kept_blocks, half, 0, :] + jnp.log2(total), LOWEST)


def half_sweep(sum_couriers, work, rounds, summed, kept, weight, live, name):
    smem = pl.BlockSpec(memory_space=pltpu.SMEM)
    vmem = pl.BlockSpec(memory_space=pltpu.VMEM)
    summed_blocks, kept_blocks = weight.shape[0], live.shape[0]

    def kernel(*refs):
        pass_kernel(sum_couriers, *refs)

    return pl.pallas_call(
        kernel,
        out_shape=jax.ShapeDtypeStruct((kept_blocks, BLOCK), jnp.float32),
        in_specs=[smem, smem] + [vmem] * 4,
        out_specs=vmem,
        scratch_shapes=pass_scratch(kept_blocks),
        compiler_params=pltpu.CompilerParams(vmem_limit_bytes=VMEM_LIMIT),
        cost_estimate=PASS_COST,
        name=name,
    )(work, rounds, summed, kept, weight, live)


PASS_COST = pl.CostEstimate(flops=28 * 2 * 512 * 512 * 128, bytes_accessed=6 << 20, transcendentals=28 * 512 * 512)


def pass_scratch(kept_blocks):
    return [
        pltpu.VMEM((HALF, 128), jnp.bfloat16),
        pltpu.VMEM((kept_blocks + 1, 2, 8, HALF), jnp.float32),
        pltpu.VMEM((kept_blocks + 1, 2, 8, HALF), jnp.float32),
    ]


def first_kernel(work_ref, rounds_ref, zone_ref, *refs):
    parts, (orders_ref, live_ref, out_ref, couriers_ref, log_cap_ref, w_ref, r_ref, m_ref, weight_ref, sem) = (
        refs[:PARTS],
        refs[PARTS:],
    )
    rows = couriers_ref.shape[0] // PARTS
    copies = [
        pltpu.make_async_copy(part, couriers_ref.at[pl.ds(i * rows, rows), :], sem.at[i]) for i, part in enumerate(parts)
    ]
    for copy in copies:
        copy.start()
    for copy in copies:
        copy.wait()
    for zone in range(ZONES):
        row = slot_of(jnp.int32(zone), zone_ref[0]) * COURIER_ROWS + BLOCK
        tail = couriers_ref[pl.ds(pl.multiple_of(row, 16), 16), :].astype(jnp.float32)
        log_cap_ref[zone : zone + 1, :] = jnp.concatenate([tail[i : i + 1] for i in range(4)], axis=1)
    cap = log_cap_ref[...]
    live = cap > 0.0
    log_cap_ref[...] = jnp.where(live, jnp.log2(jnp.where(live, cap, 1.0)), LOWEST)
    weight_ref[...] = jnp.where(live, 0.0, LOWEST)
    pass_kernel(True, work_ref, rounds_ref, couriers_ref, orders_ref, weight_ref, live_ref, out_ref, w_ref, r_ref, m_ref)


def first_half_sweep(work, rounds, zone, parts, orders, live, name):
    smem = pl.BlockSpec(memory_space=pltpu.SMEM)
    vmem = pl.BlockSpec(memory_space=pltpu.VMEM)
    return pl.pallas_call(
        first_kernel,
        out_shape=(
            jax.ShapeDtypeStruct((OB_DEV, BLOCK), jnp.float32),
            jax.ShapeDtypeStruct((ZONES * COURIER_ROWS, EMB), jnp.bfloat16),
            jax.ShapeDtypeStruct((ZONES, BLOCK), jnp.float32),
        ),
        in_specs=[smem] * 3 + [pl.BlockSpec(memory_space=pl.ANY)] * PARTS + [vmem] * 2,
        out_specs=(vmem,) * 3,
        scratch_shapes=pass_scratch(OB_DEV)
        + [pltpu.VMEM((ZONES, BLOCK), jnp.float32), pltpu.SemaphoreType.DMA((PARTS,))],
        compiler_params=pltpu.CompilerParams(vmem_limit_bytes=VMEM_LIMIT),
        cost_estimate=PASS_COST,
        name=name,
    )(work, rounds, zone.reshape(1), *parts, orders, live)


def shards(
    order_features,
    w_in,
    bias_in,
    w_out,
    bias_out,
    courier_embed,
    courier_cap,
    adjacency,
    order_count,
    courier_count,
):
    sub = lax.axis_index("sub")
    positions = jnp.arange(BLOCK, dtype=jnp.int32)

    own_live = positions < courier_count[0]
    tail = jnp.where(own_live, courier_cap, 0).reshape(4, EMB)
    block = jnp.concatenate([courier_embed, jnp.pad(tail, ((0, 12), (0, 0)))], axis=0)
    row = gather_row(block)
    row, bias_in, adjacency, order_count = lax.optimization_barrier((row, bias_in, adjacency, order_count))
    orders = embed_orders(order_features, w_in, bias_in, w_out, bias_out)
    parts, orders = gather_plane(row, orders)

    mine = adjacency % SUBS == sub
    order_live = positions[None, :] < order_count[:, None]
    order_here = jnp.where(order_live & jnp.any(mine, axis=1, keepdims=True), 0.0, LOWEST)

    def order_dual_of(partial):
        return jnp.where(order_live, -join_subs(partial), LOWEST)

    work, rounds = work_list(adjacency, order_count, jnp.ones((ZONES,), jnp.int32), "first_list")
    partial, couriers, log_cap = first_half_sweep(
        work, rounds, lax.axis_index("zone"), parts, orders, order_here, "orders_1"
    )
    courier_live = log_cap > 0.5 * LOWEST
    work, rounds = work_list(adjacency, order_count, courier_live[:, HALF].astype(jnp.int32), "work_list")
    named = jnp.any(
        (adjacency.reshape(-1)[None, :] == jnp.arange(ZONES)[:, None] * SUBS + sub), axis=1, keepdims=True
    )
    courier_here = jnp.where(courier_live & named, 0.0, LOWEST)

    def courier_pass(order_dual, name):
        return half_sweep(False, work, rounds, orders, couriers, order_dual, courier_here, name)

    order_dual = order_dual_of(partial)
    sums = join_zones(courier_pass(order_dual, "couriers_1"))
    courier_dual = jnp.where(courier_live, log_cap - sums, LOWEST)
    order_dual = order_dual_of(half_sweep(True, work, rounds, couriers, orders, courier_dual, order_here, "orders_2"))
    partial = courier_pass(order_dual, "couriers_2")
    parts = lax.all_to_all(partial, "zone", 0, 0, tiled=True)
    highest = jnp.max(parts, axis=0)
    total = highest + jnp.log2(jnp.sum(jnp.exp2(parts - highest[None]), axis=0))
    own_log_cap = jnp.log2(courier_cap.astype(jnp.float32))
    courier_out = jnp.where(own_live, DUAL_SCALE * (own_log_cap - total), 0.0)
    order_out = jnp.where(order_live, DUAL_SCALE * order_dual, 0.0)
    return order_out.reshape(-1), courier_out


def solution(mesh):
    return jax.shard_map(
        shards,
        mesh=mesh,
        in_specs=(
            P("zone", None),
            P(),
            P(),
            P(),
            P(),
            P(("zone", "sub"), None),
            P(("zone", "sub")),
            P("zone", None),
            P("zone"),
            P(("zone", "sub")),
        ),
        out_specs=(P("zone"), P(("zone", "sub"))),
        check_vma=False,
    )
```

profile of v0, /device:TPU:1, one launch (start us, length us, event | category | flops | bytes accessed | tf_op | source)
XLA Modules:
  0.0 225.9 jit_solution(694079613348294914)
XLA Ops:
  3.8 2.2 collective-permute-start
  6.0 2.6 %collective-permute-start.1 = (bf16[528,128]{1,0:T(8,128)(2,1)S(1)}, bf16[528,128]{1,0:T(8,128)(2,1)S(1)}, u32[]{:S(2)}, u32[]{:S(2)}) collective-permute-start(bf16[528,128]{1,0:T(8,128)(2,1)S(1)} %pad_maximum_fusion), channel_id=1, source_target_pairs={{0,16},{4,68},{8,24},{12,76},{16,0},{20,84},{24,8},{28,92},{32,48}... | collective-permute-start | bytes 405512 | tf_op jit(solution)/shard_map/ppermute | solution.py:55
  10.2 2.6 %collective-permute-done.1 = bf16[528,128]{1,0:T(8,128)(2,1)S(1)} collective-permute-done((bf16[528,128]{1,0:T(8,128)(2,1)S(1)}, bf16[528,128]{1,0:T(8,128)(2,1)S(1)}, u32[]{:S(2)}, u32[]{:S(2)}) %collective-permute-start.1) | collective-permute-done | bytes 135200 | tf_op jit(solution)/shard_map/ppermute | solution.py:55
  12.8 2.5 %collective-permute-start.5 = (bf16[2112,128]{1,0:T(8,128)(2,1)S(1)}, bf16[2112,128]{1,0:T(8,128)(2,1)S(1)}, u32[]{:S(2)}, u32[]{:S(2)}) collective-permute-start(bf16[2112,128]{1,0:T(8,128)(2,1)S(1)} %constant_dynamic-update-slice_fusion.refs_0_), channel_id=1, source_target_pairs={{0,96},{4,28},{8,104},{12,4},{16,112},{20,12},{24,120},{28,20},{32... | collective-permute-start | bytes 1622024 | tf_op jit(solution)/shard_map/ppermute | solution.py:55
  16.5 2.8 %collective-permute-start.6 = (bf16[2112,128]{1,0:T(8,128)(2,1)S(1)}, bf16[2112,128]{1,0:T(8,128)(2,1)S(1)}, u32[]{:S(2)}, u32[]{:S(2)}) collective-permute-start(bf16[2112,128]{1,0:T(8,128)(2,1)S(1)} %constant_dynamic-update-slice_fusion.refs_0_), channel_id=1, source_target_pairs={{0,4},{4,0},{8,12},{12,8},{16,20},{20,16},{24,28},{28,24},{32,36},... | collective-permute-start | bytes 1622024 | tf_op jit(solution)/shard_map/ppermute | solution.py:43
  21.0 6.6 %embed_orders.1.refs_8_.refs_2_.refs_3_ = bf16[8192,128]{1,0:T(8,128)(2,1)S(1)} custom-call(bf16[8192,128]{1,0:T(8,128)(2,1)} %x_hbm.1, bf16[128,512]{1,0:T(8,128)(2,1)} %w_in_hbm.1, f32[1,512]{1,0:T(1,128)} %bitcast.22, bf16[512,128]{1,0:T(8,128)(2,1)} %w_out_hbm.1, f32[1,128]{1,0:T(1,128)} %bitcast.23), custom_call_target="tpu_custom_call" | custom-call | flops 2147483648 | bytes 4194304 | tf_op jit(solution)/shard_map/embed_orders/pallas_call | solution.py:139
  27.7 3.5 %collective-permute-done.3.refs_1_ = bf16[2112,128]{1,0:T(8,128)(2,1)S(1)} collective-permute-done((bf16[2112,128]{1,0:T(8,128)(2,1)S(1)}, bf16[2112,128]{1,0:T(8,128)(2,1)S(1)}, u32[]{:S(2)}, u32[]{:S(2)}) %collective-permute-start.3) | collective-permute-done | bytes 540704 | tf_op jit(solution)/shard_map/ppermute | solution.py:55
  31.2 3.2 %collective-permute-start.7 = (bf16[2112,128]{1,0:T(8,128)(2,1)S(1)}, bf16[2112,128]{1,0:T(8,128)(2,1)S(1)}, u32[]{:S(2)}, u32[]{:S(2)}) collective-permute-start(bf16[2112,128]{1,0:T(8,128)(2,1)S(1)} %collective-permute-done.3.refs_1_), channel_id=1, source_target_pairs={{0,4},{4,0},{8,12},{12,8},{16,20},{20,16},{24,28},{28,24},{32,36},... | collective-permute-start | bytes 1622024 | tf_op jit(solution)/shard_map/ppermute | solution.py:43
  34.9 2.2 first_list.1
  37.5 39.1 %orders_1.1 = (f32[16,512]{1,0:T(8,128)S(1)}, bf16[16896,128]{1,0:T(8,128)(2,1)S(1)}, f32[32,512]{1,0:T(8,128)S(1)}) custom-call(s32[272]{0:T(512)S(1)} %get-tuple-element.19.work_ref, s32[1]{0:T(128)} %get-tuple-element.20.rounds_ref, s32[1]{0:T(128)} %bitcast.2.zone_ref, bf16[2112,128]{1,0:T(8,128)(2,1)S(1)} %constant_dynamic-update-slice_fusion.refs_0_, ...), custom_call_target="tpu_custom_call" | custom-call | flops 1879048192 | bytes 6291456 | tf_op jit(solution)/shard_map/orders_1/pallas_call | solution.py:355
  76.6 3.8 %collective-permute-start.12 = (f32[16,512]{1,0:T(8,128)S(1)}, f32[16,512]{1,0:T(8,128)S(1)}, u32[]{:S(2)}, u32[]{:S(2)}) collective-permute-start(f32[16,512]{1,0:T(8,128)S(1)} %get-tuple-element.31), channel_id=1, source_target_pairs={{0,3},{1,0},{2,1},{3,2},{4,7},{5,4},{6,5},{7,6},{8,11},{9,8},{10,9... | collective-permute-start | bytes 98312 | tf_op jit(solution)/shard_map/ppermute | solution.py:47
  80.4 1.9 collective-permute-start.11
  83.2 2.2 work_list.1
  86.3 33.6 %couriers_1.1 = f32[32,512]{1,0:T(8,128)S(1)} custom-call(s32[272]{0:T(512)S(1)} %get-tuple-element.28.refs_0_, s32[1]{0:T(128)} %get-tuple-element.29.refs_1_, bf16[8192,128]{1,0:T(8,128)(2,1)S(1)} %embed_orders.1.refs_8_.refs_2_.refs_3_, bf16[16896,128]{1,0:T(8,128)(2,1)S(1)} %get-tuple-element.30.refs_3_.refs_2_, ...), custom_call_target="tpu_custom_call" | custom-call | flops 1879048192 | bytes 6291456 | tf_op jit(solution)/shard_map/couriers_1/pallas_call | solution.py:305
  121.5 1.4 collective-permute-start.14
  122.9 1.9 collective-permute-done.16
  127.0 5.7 %collective-permute-start.19 = (f32[32,512]{1,0:T(8,128)S(1)}, f32[32,512]{1,0:T(8,128)S(1)}, u32[]{:S(2)}, u32[]{:S(2)}) collective-permute-start(f32[32,512]{1,0:T(8,128)S(1)} %multiply_add_fusion), channel_id=1, source_target_pairs={{0,96},{4,28},{8,104},{12,4},{16,112},{20,12},{24,120},{28,20},{32... | collective-permute-start | bytes 196616 | tf_op jit(solution)/shard_map/ppermute | solution.py:55
  134.6 2.8 %collective-permute-done.18 = f32[32,512]{1,0:T(8,128)S(1)} collective-permute-done((f32[32,512]{1,0:T(8,128)S(1)}, f32[32,512]{1,0:T(8,128)S(1)}, u32[]{:S(2)}, u32[]{:S(2)}) %collective-permute-start.18) | collective-permute-done | bytes 65568 | tf_op jit(solution)/shard_map/ppermute | solution.py:55
  137.8 33.4 %orders_2.1 = f32[16,512]{1,0:T(8,128)S(1)} custom-call(s32[272]{0:T(512)S(1)} %get-tuple-element.28.refs_0_, s32[1]{0:T(128)} %get-tuple-element.29.refs_1_, bf16[16896,128]{1,0:T(8,128)(2,1)S(1)} %get-tuple-element.30.refs_3_.refs_2_, bf16[8192,128]{1,0:T(8,128)(2,1)S(1)} %embed_orders.1.refs_8_.refs_2_.refs_3_, ...), custom_call_target="tpu_custom_call" | custom-call | flops 1879048192 | bytes 6291456 | tf_op jit(solution)/shard_map/orders_2/pallas_call | solution.py:305
  171.4 1.4 collective-permute-start.20
  172.7 1.6 collective-permute-done.22
  176.5 33.4 %couriers_2.1 = f32[32,512]{1,0:T(8,128)S(1)} custom-call(s32[272]{0:T(512)S(1)} %get-tuple-element.28.refs_0_, s32[1]{0:T(128)} %get-tuple-element.29.refs_1_, bf16[8192,128]{1,0:T(8,128)(2,1)S(1)} %embed_orders.1.refs_8_.refs_2_.refs_3_, bf16[16896,128]{1,0:T(8,128)(2,1)S(1)} %get-tuple-element.30.refs_3_.refs_2_, ...), custom_call_target="tpu_custom_call" | custom-call | flops 1879048192 | bytes 6291456 | tf_op jit(solution)/shard_map/couriers_2/pallas_call | solution.py:305
  210.6 7.2 %all-to-all-start = ((f32[32,1,512]{2,1,0:T(1,128)}), f32[32,1,512]{2,1,0:T(1,128)S(1)}, u32[]{:S(2)}, u32[]{:S(2)}) async-start(f32[32,1,512]{2,1,0:T(1,128)} %copy.17), calls=%async_computation | async-start | bytes 131072 | tf_op jit(solution)/shard_map/all_to_all | solution.py:421
  218.5 6.7 %all-to-all-done = f32[32,1,512]{2,1,0:T(1,128)S(1)} async-done(((f32[32,1,512]{2,1,0:T(1,128)}), f32[32,1,512]{2,1,0:T(1,128)S(1)}, u32[]{:S(2)}, u32[]{:S(2)}) %all-to-all-start) | async-done | bytes 65568 | tf_op jit(solution)/shard_map/all_to_all | solution.py:421
  (67 shorter events, 20.0 us)
Async XLA Ops:
  3.8 6.3 %collective-permute-start = (bf16[528,128]{1,0:T(8,128)(2,1)S(1)}, bf16[528,128]{1,0:T(8,128)(2,1)S(1)}, u32[]{:S(2)}, u32[]{:S(2)}) collective-permute-start(bf16[528,128]{1,0:T(8,128)(2,1)S(1)} %pad_maximum_fusion), channel_id=1, source_target_pairs={{0,8},{4,36},{8,16},{12,44},{16,24},{20,52},{24,0},{28,60},{32,40}... | collective-permute-start | bytes 405512 | tf_op jit(solution)/shard_map/ppermute | solution.py:55
  6.0 6.8 %collective-permute-start.1 = (bf16[528,128]{1,0:T(8,128)(2,1)S(1)}, bf16[528,128]{1,0:T(8,128)(2,1)S(1)}, u32[]{:S(2)}, u32[]{:S(2)}) collective-permute-start(bf16[528,128]{1,0:T(8,128)(2,1)S(1)} %pad_maximum_fusion), channel_id=1, source_target_pairs={{0,16},{4,68},{8,24},{12,76},{16,0},{20,84},{24,8},{28,92},{32,48}... | collective-permute-start | bytes 405512 | tf_op jit(solution)/shard_map/ppermute | solution.py:55
  8.6 4.2 %collective-permute-start.2 = (bf16[528,128]{1,0:T(8,128)(2,1)S(1)}, bf16[528,128]{1,0:T(8,128)(2,1)S(1)}, u32[]{:S(2)}, u32[]{:S(2)}) collective-permute-start(bf16[528,128]{1,0:T(8,128)(2,1)S(1)} %pad_maximum_fusion), channel_id=1, source_target_pairs={{0,24},{4,100},{8,0},{12,108},{16,8},{20,116},{24,16},{28,124},{32... | collective-permute-start | bytes 405512 | tf_op jit(solution)/shard_map/ppermute | solution.py:55
  12.8 14.8 %collective-permute-start.5 = (bf16[2112,128]{1,0:T(8,128)(2,1)S(1)}, bf16[2112,128]{1,0:T(8,128)(2,1)S(1)}, u32[]{:S(2)}, u32[]{:S(2)}) collective-permute-start(bf16[2112,128]{1,0:T(8,128)(2,1)S(1)} %constant_dynamic-update-slice_fusion.refs_0_), channel_id=1, source_target_pairs={{0,96},{4,28},{8,104},{12,4},{16,112},{20,12},{24,120},{28,20},{32... | collective-permute-start | bytes 1622024 | tf_op jit(solution)/shard_map/ppermute | solution.py:55
  15.4 12.3 %collective-permute-start.4 = (bf16[2112,128]{1,0:T(8,128)(2,1)S(1)}, bf16[2112,128]{1,0:T(8,128)(2,1)S(1)}, u32[]{:S(2)}, u32[]{:S(2)}) collective-permute-start(bf16[2112,128]{1,0:T(8,128)(2,1)S(1)} %constant_dynamic-update-slice_fusion.refs_0_), channel_id=1, source_target_pairs={{0,64},{4,20},{8,72},{12,28},{16,80},{20,4},{24,88},{28,12},{32,96... | collective-permute-start | bytes 1622024 | tf_op jit(solution)/shard_map/ppermute | solution.py:55
  15.9 15.3 %collective-permute-start.3 = (bf16[2112,128]{1,0:T(8,128)(2,1)S(1)}, bf16[2112,128]{1,0:T(8,128)(2,1)S(1)}, u32[]{:S(2)}, u32[]{:S(2)}) collective-permute-start(bf16[2112,128]{1,0:T(8,128)(2,1)S(1)} %constant_dynamic-update-slice_fusion.refs_0_), channel_id=1, source_target_pairs={{0,32},{4,12},{8,40},{12,20},{16,48},{20,28},{24,56},{28,4},{32,64... | collective-permute-start | bytes 1622024 | tf_op jit(solution)/shard_map/ppermute | solution.py:55
  16.5 20.9 %collective-permute-start.6 = (bf16[2112,128]{1,0:T(8,128)(2,1)S(1)}, bf16[2112,128]{1,0:T(8,128)(2,1)S(1)}, u32[]{:S(2)}, u32[]{:S(2)}) collective-permute-start(bf16[2112,128]{1,0:T(8,128)(2,1)S(1)} %constant_dynamic-update-slice_fusion.refs_0_), channel_id=1, source_target_pairs={{0,4},{4,0},{8,12},{12,8},{16,20},{20,16},{24,28},{28,24},{32,36},... | collective-permute-start | bytes 1622024 | tf_op jit(solution)/shard_map/ppermute | solution.py:43
  31.2 6.2 %collective-permute-start.7 = (bf16[2112,128]{1,0:T(8,128)(2,1)S(1)}, bf16[2112,128]{1,0:T(8,128)(2,1)S(1)}, u32[]{:S(2)}, u32[]{:S(2)}) collective-permute-start(bf16[2112,128]{1,0:T(8,128)(2,1)S(1)} %collective-permute-done.3.refs_1_), channel_id=1, source_target_pairs={{0,4},{4,0},{8,12},{12,8},{16,20},{20,16},{24,28},{28,24},{32,36},... | collective-permute-start | bytes 1622024 | tf_op jit(solution)/shard_map/ppermute | solution.py:43
  34.4 3.0 %collective-permute-start.8 = (bf16[2112,128]{1,0:T(8,128)(2,1)S(1)}, bf16[2112,128]{1,0:T(8,128)(2,1)S(1)}, u32[]{:S(2)}, u32[]{:S(2)}) collective-permute-start(bf16[2112,128]{1,0:T(8,128)(2,1)S(1)} %collective-permute-done.4.refs_2_), channel_id=1, source_target_pairs={{0,4},{4,0},{8,12},{12,8},{16,20},{20,16},{24,28},{28,24},{32,36},... | collective-permute-start | bytes 1622024 | tf_op jit(solution)/shard_map/ppermute | solution.py:43
  34.4 3.1 %collective-permute-start.9 = (bf16[2112,128]{1,0:T(8,128)(2,1)S(1)}, bf16[2112,128]{1,0:T(8,128)(2,1)S(1)}, u32[]{:S(2)}, u32[]{:S(2)}) collective-permute-start(bf16[2112,128]{1,0:T(8,128)(2,1)S(1)} %collective-permute-done.5.refs_3_), channel_id=1, source_target_pairs={{0,4},{4,0},{8,12},{12,8},{16,20},{20,16},{24,28},{28,24},{32,36},... | collective-permute-start | bytes 1622024 | tf_op jit(solution)/shard_map/ppermute | solution.py:43
  76.6 8.8 %collective-permute-start.12 = (f32[16,512]{1,0:T(8,128)S(1)}, f32[16,512]{1,0:T(8,128)S(1)}, u32[]{:S(2)}, u32[]{:S(2)}) collective-permute-start(f32[16,512]{1,0:T(8,128)S(1)} %get-tuple-element.31), channel_id=1, source_target_pairs={{0,3},{1,0},{2,1},{3,2},{4,7},{5,4},{6,5},{7,6},{8,11},{9,8},{10,9... | collective-permute-start | bytes 98312 | tf_op jit(solution)/shard_map/ppermute | solution.py:47
  80.4 5.0 %collective-permute-start.11 = (f32[16,512]{1,0:T(8,128)S(1)}, f32[16,512]{1,0:T(8,128)S(1)}, u32[]{:S(2)}, u32[]{:S(2)}) collective-permute-start(f32[16,512]{1,0:T(8,128)S(1)} %get-tuple-element.31), channel_id=1, source_target_pairs={{0,2},{1,3},{2,0},{3,1},{4,6},{5,7},{6,4},{7,5},{8,10},{9,11},{10,... | collective-permute-start | bytes 98312 | tf_op jit(solution)/shard_map/ppermute | solution.py:47
  82.3 4.0 %collective-permute-start.10 = (f32[16,512]{1,0:T(8,128)S(1)}, f32[16,512]{1,0:T(8,128)S(1)}, u32[]{:S(2)}, u32[]{:S(2)}) collective-permute-start(f32[16,512]{1,0:T(8,128)S(1)} %get-tuple-element.31), channel_id=1, source_target_pairs={{0,1},{1,2},{2,3},{3,0},{4,5},{5,6},{6,7},{7,4},{8,9},{9,10},{10,1... | collective-permute-start | bytes 98312 | tf_op jit(solution)/shard_map/ppermute | solution.py:47
  119.9 1.3 collective-permute-start.13
  121.3 3.5 %collective-permute-start.16 = (f32[32,512]{1,0:T(8,128)S(1)}, f32[32,512]{1,0:T(8,128)S(1)}, u32[]{:S(2)}, u32[]{:S(2)}) collective-permute-start(f32[32,512]{1,0:T(8,128)S(1)} %multiply_add_fusion.1), channel_id=1, source_target_pairs={{0,24},{4,100},{8,0},{12,108},{16,8},{20,116},{24,16},{28,124},{32... | collective-permute-start | bytes 196616 | tf_op jit(solution)/shard_map/ppermute | solution.py:55
  121.4 4.7 %collective-permute-start.15 = (f32[32,512]{1,0:T(8,128)S(1)}, f32[32,512]{1,0:T(8,128)S(1)}, u32[]{:S(2)}, u32[]{:S(2)}) collective-permute-start(f32[32,512]{1,0:T(8,128)S(1)} %multiply_add_fusion.1), channel_id=1, source_target_pairs={{0,16},{4,68},{8,24},{12,76},{16,0},{20,84},{24,8},{28,92},{32,48}... | collective-permute-start | bytes 196616 | tf_op jit(solution)/shard_map/ppermute | solution.py:55
  121.5 5.4 %collective-permute-start.14 = (f32[32,512]{1,0:T(8,128)S(1)}, f32[32,512]{1,0:T(8,128)S(1)}, u32[]{:S(2)}, u32[]{:S(2)}) collective-permute-start(f32[32,512]{1,0:T(8,128)S(1)} %multiply_add_fusion.1), channel_id=1, source_target_pairs={{0,8},{4,36},{8,16},{12,44},{16,24},{20,52},{24,0},{28,60},{32,40}... | collective-permute-start | bytes 196616 | tf_op jit(solution)/shard_map/ppermute | solution.py:55
  127.0 7.6 %collective-permute-start.19 = (f32[32,512]{1,0:T(8,128)S(1)}, f32[32,512]{1,0:T(8,128)S(1)}, u32[]{:S(2)}, u32[]{:S(2)}) collective-permute-start(f32[32,512]{1,0:T(8,128)S(1)} %multiply_add_fusion), channel_id=1, source_target_pairs={{0,96},{4,28},{8,104},{12,4},{16,112},{20,12},{24,120},{28,20},{32... | collective-permute-start | bytes 196616 | tf_op jit(solution)/shard_map/ppermute | solution.py:55
  132.7 4.7 %collective-permute-start.18 = (f32[32,512]{1,0:T(8,128)S(1)}, f32[32,512]{1,0:T(8,128)S(1)}, u32[]{:S(2)}, u32[]{:S(2)}) collective-permute-start(f32[32,512]{1,0:T(8,128)S(1)} %multiply_add_fusion), channel_id=1, source_target_pairs={{0,64},{4,20},{8,72},{12,28},{16,80},{20,4},{24,88},{28,12},{32,96... | collective-permute-start | bytes 196616 | tf_op jit(solution)/shard_map/ppermute | solution.py:55
  132.7 5.0 %collective-permute-start.17 = (f32[32,512]{1,0:T(8,128)S(1)}, f32[32,512]{1,0:T(8,128)S(1)}, u32[]{:S(2)}, u32[]{:S(2)}) collective-permute-start(f32[32,512]{1,0:T(8,128)S(1)} %multiply_add_fusion), channel_id=1, source_target_pairs={{0,32},{4,12},{8,40},{12,20},{16,48},{20,28},{24,56},{28,4},{32,64... | collective-permute-start | bytes 196616 | tf_op jit(solution)/shard_map/ppermute | solution.py:55
  171.2 3.1 %collective-permute-start.22 = (f32[16,512]{1,0:T(8,128)S(1)}, f32[16,512]{1,0:T(8,128)S(1)}, u32[]{:S(2)}, u32[]{:S(2)}) collective-permute-start(f32[16,512]{1,0:T(8,128)S(1)} %orders_2.1), channel_id=1, source_target_pairs={{0,3},{1,0},{2,1},{3,2},{4,7},{5,4},{6,5},{7,6},{8,11},{9,8},{10,9... | collective-permute-start | bytes 98312 | tf_op jit(solution)/shard_map/ppermute | solution.py:47
  171.3 4.4 %collective-permute-start.21 = (f32[16,512]{1,0:T(8,128)S(1)}, f32[16,512]{1,0:T(8,128)S(1)}, u32[]{:S(2)}, u32[]{:S(2)}) collective-permute-start(f32[16,512]{1,0:T(8,128)S(1)} %orders_2.1), channel_id=1, source_target_pairs={{0,2},{1,3},{2,0},{3,1},{4,6},{5,7},{6,4},{7,5},{8,10},{9,11},{10,... | collective-permute-start | bytes 98312 | tf_op jit(solution)/shard_map/ppermute | solution.py:47
  171.4 5.1 %collective-permute-start.20 = (f32[16,512]{1,0:T(8,128)S(1)}, f32[16,512]{1,0:T(8,128)S(1)}, u32[]{:S(2)}, u32[]{:S(2)}) collective-permute-start(f32[16,512]{1,0:T(8,128)S(1)} %orders_2.1), channel_id=1, source_target_pairs={{0,1},{1,2},{2,3},{3,0},{4,5},{5,6},{6,7},{7,4},{8,9},{9,10},{10,1... | collective-permute-start | bytes 98312 | tf_op jit(solution)/shard_map/ppermute | solution.py:47
  210.6 14.5 %all-to-all-start = ((f32[32,1,512]{2,1,0:T(1,128)}), f32[32,1,512]{2,1,0:T(1,128)S(1)}, u32[]{:S(2)}, u32[]{:S(2)}) async-start(f32[32,1,512]{2,1,0:T(1,128)} %copy.17), calls=%async_computation | async-start | bytes 131072 | tf_op jit(solution)/shard_map/all_to_all | solution.py:421
  (3 other events, 81.2 us)
where the time goes:
time: 224 us; the launch traced here: 226 us
  Pallas kernels  150 us (67%)
  starting transfers between devices  39.3 us (18%)
  waiting for transfers between devices  27.5 us (12%)
  other arithmetic  3.8 us (2%)
  local copies, waits for them, and re-layouts  3.33 us (1%)
    pallas_call x3, Pallas kernels, half_sweep(): pl.pallas_call(kernel, out_shape=jax.ShapeDtypeStruct((kept_blocks, BLOCK...  100 us
    pallas_call x1, Pallas kernels, first_half_sweep(): pl.pallas_call(first_kernel, out_shape=(jax.ShapeDtypeStruct((OB_DEV, BLO...  39.1 us
    ppermute x12, starting transfers between devices, plane_step(): return lax.ppermute(value, 'zone', pairs)  17.4 us
    ppermute x12, waiting for transfers between devices, plane_step(): return lax.ppermute(value, 'zone', pairs)  14.9 us
    ppermute x6, starting transfers between devices, along_z(): lax.ppermute(value, 'sub', [(i, (i + step) % SUBS) for i in range(SUBS)])  7.98 us
    all_to_all x1, starting transfers between devices, shards(): parts = lax.all_to_all(partial, 'zone', 0, 0, tiled=True)  7.22 us
    all_to_all x1, waiting for transfers between devices, shards(): parts = lax.all_to_all(partial, 'zone', 0, 0, tiled=True)  6.7 us
    ppermute x5, starting transfers between devices, other_core(): lax.ppermute(value, 'zone', [(zone_of(y, x, c), zone_of(y, x, 1 - c)) for...  6.66 us
  transfers between devices with their start and end apart: 24, of which 16 were waited for; matrix products, arithmetic and copies ran while one was open for 1% of the time, Pallas kernels for 5%

commit v1 on v0

--- a/solution.py
+++ b/solution.py
@@ -29,7 +29,6 @@
 DUAL_SCALE = TEMPER * math.log(2.0)
 
 VMEM_LIMIT = 16 * 1024 * 1024
-PARTS = 8
 
 
 def zone_of(y, x, core):
@@ -59,11 +58,8 @@
     return jnp.concatenate([block] + [plane_step(block, 0, step) for step in (1, 2, 3)], axis=0)
 
 
-def gather_plane(row, meanwhile):
-    own = [row] + [plane_step(row, 1, step) for step in (1, 2, 3)]
-    swapped = [other_core(row)]
-    own[1], own[2], own[3], meanwhile = lax.optimization_barrier((own[1], own[2], own[3], meanwhile))
-    return own + swapped + [other_core(part) for part in own[1:]], meanwhile
+PARTS = 8
+EARLY = (0, 2, 3, 4)
 
 
 def slot_of(zone, me):
@@ -73,6 +69,13 @@
     first = jnp.where(odd == 0, back_x, back_y)
     second = jnp.where(odd == 0, back_y, back_x)
     return ((me ^ zone) & 1) * 16 + second * 4 + first
+
+
+def early_slot(slot):
+    part = slot >> 2
+    index = sum(jnp.where(part == p, i, 0) for i, p in enumerate(EARLY))
+    is_early = sum(jnp.where(part == p, 1, 0) for p in EARLY)
+    return is_early, index * 4 + (slot & 3)
 
 
 def join(*parts):
@@ -173,27 +176,68 @@
     rounds_ref[0] = (n + REST - 1) // REST
 
 
-def work_list(adjacency, order_count, courier_two, name):
-    zone, sub = lax.axis_index("zone"), lax.axis_index("sub")
+def first_list_kernel(pair_ref, early_ref, late_ref, early_rounds_ref, late_rounds_ref, has_ref):
+    def one_block(b, counts):
+        early_n, late_n = counts
+        early_any, late_any = jnp.int32(0), jnp.int32(0)
+        for i in range(ADJ):
+            e = pair_ref[b * ADJ + i]
+            early = (e >> 24) & 1
+            late = (e >> 25) & 1
+            two = (e >> 26) & 1
+            e = e & 0xFFFFFF
+            early_any, late_any = early_any | early, late_any | late
+            for step, more in ((0, 1), (257, 1), (65536, two), (65536 + 257, two)):
+                early_ref[early_n] = e + step
+                late_ref[late_n] = e + step
+                early_n = early_n + (early & more)
+                late_n = late_n + (late & more)
+        has_ref[b] = early_any
+        has_ref[OB_DEV + b] = late_any
+        return early_n, late_n
+
+    counts = lax.fori_loop(0, OB_DEV, one_block, (jnp.int32(0), jnp.int32(0)))
+    for n, list_ref, rounds_ref in ((counts[0], early_ref, early_rounds_ref), (counts[1], late_ref, late_rounds_ref)):
+        for i in range(REST):
+            list_ref[n + i] = jnp.int32(NO_ORDER * 65536 + NO_COURIER * 256)
+        rounds_ref[0] = (n + REST - 1) // REST
+
+
+def call_on_scalars(kernel, sizes, name, *operands):
+    smem = pl.BlockSpec(memory_space=pltpu.SMEM)
+    return pl.pallas_call(
+        kernel,
+        out_shape=tuple(jax.ShapeDtypeStruct((size,), jnp.int32) for size in sizes),
+        in_specs=[smem] * len(operands),
+        out_specs=(smem,) * len(sizes),
+        compiler_params=pltpu.CompilerParams(vmem_limit_bytes=1024 * 1024),
+        name=name,
+    )(*operands)
+
+
+def pair_fields(adjacency, order_count):
     flat = adjacency.reshape(-1)
     z = flat >> 2
-    mine = jnp.where((flat & 3) == sub, 1, 0)
+    mine = jnp.where((flat & 3) == lax.axis_index("sub"), 1, 0)
     two = jnp.repeat(jnp.where(order_count > HALF, 1, 0), ADJ)
     block = jnp.arange(OB_DEV * ADJ, dtype=jnp.int32) // ADJ
-    entry = (2 * block << 16) + (2 * z << 8) + 2 * slot_of(z, zone)
-    pairs = entry + (mine << 24) + ((mine * two) << 25)
-    smem = pl.BlockSpec(memory_space=pltpu.SMEM)
-    return pl.pallas_call(
-        list_kernel,
-        out_shape=(
-            jax.ShapeDtypeStruct((LIST_SIZE,), jnp.int32),
-            jax.ShapeDtypeStruct((1,), jnp.int32),
-        ),
-        in_specs=[smem] * 2,
-        out_specs=(smem, smem),
-        compiler_params=pltpu.CompilerParams(vmem_limit_bytes=1024 * 1024),
-        name=name,
-    )(pairs.astype(jnp.int32), courier_two)
+    slot = slot_of(z, lax.axis_index("zone"))
+    return (2 * block << 16) + (2 * z << 8), slot, mine, two
+
+
+def first_lists(adjacency, order_count):
+    entry, slot, mine, two = pair_fields(adjacency, order_count)
+    is_early, place = early_slot(slot)
+    entry = entry + 2 * jnp.where(is_early == 1, place, slot)
+    pairs = entry + ((mine & is_early) << 24) + ((mine & (1 - is_early)) << 25) + (two << 26)
+    sizes = (LIST_SIZE, LIST_SIZE, 1, 1, 2 * OB_DEV)
+    return call_on_scalars(first_list_kernel, sizes, "first_lists", pairs.astype(jnp.int32))
+
+
+def work_list(adjacency, order_count, courier_two):
+    entry, slot, mine, two = pair_fields(adjacency, order_count)
+    pairs = entry + 2 * slot + (mine << 24) + ((mine * two) << 25)
+    return call_on_scalars(list_kernel, (LIST_SIZE, 1), "work_list", pairs.astype(jnp.int32), courier_two)
 
 
 def pass_kernel(sum_couriers, list_ref, rounds_ref, summed_ref, kept_ref, weight_ref, live_ref, out_ref, w_ref, r_ref, m_ref):
@@ -325,48 +369,66 @@
     ]
 
 
-def first_kernel(work_ref, rounds_ref, zone_ref, *refs):
-    parts, (orders_ref, live_ref, out_ref, couriers_ref, log_cap_ref, w_ref, r_ref, m_ref, weight_ref, sem) = (
-        refs[:PARTS],
-        refs[PARTS:],
+def first_kernel(early, work_ref, rounds_ref, zone_ref, has_ref, *refs):
+    count = len(EARLY) if early else PARTS
+    parts, (orders_ref, live_ref, out_ref, couriers_ref, log_cap_ref, w_ref, r_ref, m_ref, weight_ref, here_ref, sem) = (
+        refs[:count],
+        refs[count:],
     )
-    rows = couriers_ref.shape[0] // PARTS
+    rows = couriers_ref.shape[0] // count
     copies = [
         pltpu.make_async_copy(part, couriers_ref.at[pl.ds(i * rows, rows), :], sem.at[i]) for i, part in enumerate(parts)
     ]
     for copy in copies:
         copy.start()
+    for block in range(OB_DEV):
+        named = has_ref[block if early else OB_DEV + block] > 0
+        here_ref[block : block + 1, :] = jnp.where(named, live_ref[block : block + 1, :], LOWEST)
     for copy in copies:
         copy.wait()
     for zone in range(ZONES):
-        row = slot_of(jnp.int32(zone), zone_ref[0]) * COURIER_ROWS + BLOCK
+        slot = slot_of(jnp.int32(zone), zone_ref[0])
+        if early:
+            _, slot = early_slot(slot)
+        row = slot * COURIER_ROWS + BLOCK
         tail = couriers_ref[pl.ds(pl.multiple_of(row, 16), 16), :].astype(jnp.float32)
         log_cap_ref[zone : zone + 1, :] = jnp.concatenate([tail[i : i + 1] for i in range(4)], axis=1)
     cap = log_cap_ref[...]
     live = cap > 0.0
     log_cap_ref[...] = jnp.where(live, jnp.log2(jnp.where(live, cap, 1.0)), LOWEST)
     weight_ref[...] = jnp.where(live, 0.0, LOWEST)
-    pass_kernel(True, work_ref, rounds_ref, couriers_ref, orders_ref, weight_ref, live_ref, out_ref, w_ref, r_ref, m_ref)
-
-
-def first_half_sweep(work, rounds, zone, parts, orders, live, name):
+    pass_kernel(True, work_ref, rounds_ref, couriers_ref, orders_ref, weight_ref, here_ref, out_ref, w_ref, r_ref, m_ref)
+
+
+def first_half_sweep(early, work, rounds, zone, has, parts, orders, live, name):
     smem = pl.BlockSpec(memory_space=pltpu.SMEM)
     vmem = pl.BlockSpec(memory_space=pltpu.VMEM)
+
+    def kernel(*refs):
+        first_kernel(early, *refs)
+
+    couriers = (len(parts) * 4 * COURIER_ROWS, EMB)
+    kept_out = () if early else (
+        jax.ShapeDtypeStruct(couriers, jnp.bfloat16),
+        jax.ShapeDtypeStruct((ZONES, BLOCK), jnp.float32),
+    )
+    as_scratch = [pltpu.VMEM(couriers, jnp.bfloat16), pltpu.VMEM((ZONES, BLOCK), jnp.float32)] if early else []
     return pl.pallas_call(
-        first_kernel,
-        out_shape=(
-            jax.ShapeDtypeStruct((OB_DEV, BLOCK), jnp.float32),
-            jax.ShapeDtypeStruct((ZONES * COURIER_ROWS, EMB), jnp.bfloat16),
-            jax.ShapeDtypeStruct((ZONES, BLOCK), jnp.float32),
-        ),
-        in_specs=[smem] * 3 + [pl.BlockSpec(memory_space=pl.ANY)] * PARTS + [vmem] * 2,
-        out_specs=(vmem,) * 3,
-        scratch_shapes=pass_scratch(OB_DEV)
-        + [pltpu.VMEM((ZONES, BLOCK), jnp.float32), pltpu.SemaphoreType.DMA((PARTS,))],
+        kernel,
+        out_shape=(jax.ShapeDtypeStruct((OB_DEV, BLOCK), jnp.float32),) + kept_out,
+        in_specs=[smem] * 4 + [pl.BlockSpec(memory_space=pl.ANY)] * len(parts) + [vmem] * 2,
+        out_specs=(vmem,) * (1 + len(kept_out)),
+        scratch_shapes=as_scratch
+        + pass_scratch(OB_DEV)
+        + [
+            pltpu.VMEM((ZONES, BLOCK), jnp.float32),
+            pltpu.VMEM((OB_DEV, BLOCK), jnp.float32),
+            pltpu.SemaphoreType.DMA((len(parts),)),
+        ],
         compiler_params=pltpu.CompilerParams(vmem_limit_bytes=VMEM_LIMIT),
-        cost_estimate=PASS_COST,
+        cost_estimate=pl.CostEstimate(flops=14 * 2 * 512 * 512 * 128, bytes_accessed=6 << 20, transcendentals=14 * 512 * 512),
         name=name,
-    )(work, rounds, zone.reshape(1), *parts, orders, live)
+    )(work, rounds, zone.reshape(1), has, *parts, orders, live)
 
 
 def shards(
@@ -390,21 +452,35 @@
     row = gather_row(block)
     row, bias_in, adjacency, order_count = lax.optimization_barrier((row, bias_in, adjacency, order_count))
     orders = embed_orders(order_features, w_in, bias_in, w_out, bias_out)
-    parts, orders = gather_plane(row, orders)
+    order_live = positions[None, :] < order_count[:, None]
+    live = jnp.where(order_live, 0.0, LOWEST)
+    early_list, late_list, early_rounds, late_rounds, has = first_lists(adjacency, order_count)
+    zone = lax.axis_index("zone")
+
+    own = [row] + [plane_step(row, 1, step) for step in (1, 2, 3)]
+    other = [other_core(row)] + [None] * 3
+    for step in (3, 2):
+        own[step], orders = lax.optimization_barrier((own[step], orders))
+        other[step] = other_core(own[step])
+    parts = own + other
+    (early_partial,) = first_half_sweep(
+        True, early_list, early_rounds, zone, has, [parts[p] for p in EARLY], orders, live, "orders_1_early"
+    )
+    own[1], early_partial = lax.optimization_barrier((own[1], early_partial))
+    other[1] = other_core(own[1])
+    late_partial, couriers, log_cap = first_half_sweep(
+        False, late_list, late_rounds, zone, has, own + other, orders, live, "orders_1"
+    )
+    partial = join(early_partial, late_partial)
 
     mine = adjacency % SUBS == sub
-    order_live = positions[None, :] < order_count[:, None]
     order_here = jnp.where(order_live & jnp.any(mine, axis=1, keepdims=True), 0.0, LOWEST)
 
     def order_dual_of(partial):
         return jnp.where(order_live, -join_subs(partial), LOWEST)
 
-    work, rounds = work_list(adjacency, order_count, jnp.ones((ZONES,), jnp.int32), "first_list")
-    partial, couriers, log_cap = first_half_sweep(
-        work, rounds, lax.axis_index("zone"), parts, orders, order_here, "orders_1"
-    )
     courier_live = log_cap > 0.5 * LOWEST
-    work, rounds = work_list(adjacency, order_count, courier_live[:, HALF].astype(jnp.int32), "work_list")
+    work, rounds = work_list(adjacency, order_count, courier_live[:, HALF].astype(jnp.int32))
     named = jnp.any(
         (adjacency.reshape(-1)[None, :] == jnp.arange(ZONES)[:, None] * SUBS + sub), axis=1, keepdims=True
     )

time: 224 us -> 234 us (1.045); the launches traced: 226 us -> 232 us
  starting transfers between devices: 39.3 us -> 91.1 us
  Pallas kernels: 150 us -> 106 us
    pallas_call x3, Pallas kernels: 100 us -> 63.2 us  [half_sweep(): pl.pallas_call(kernel, out_shape=jax.ShapeDtypeStruct((kept_blocks, BLOCK...]
    ppermute x6, starting transfers between devices: 7.98 us -> 27 us  [along_z(): lax.ppermute(value, 'sub', [(i, (i + step) % SUBS) for i in range(SUBS)])]
    all_to_all x1, starting transfers between devices: 7.22 us -> 25.7 us  [shards(): parts = lax.all_to_all(partial, 'zone', 0, 0, tiled=True)]
    ppermute x12, starting transfers between devices: 17.4 us -> 30.1 us  [plane_step(): return lax.ppermute(value, 'zone', pairs)]
    pallas_call x3 -> x4, Pallas kernels: 43.4 us -> 36.4 us  [the longest x2 31.6 us: first_half_sweep(): pl.pallas_call(kernel, out_shape=(jax.ShapeDtypeStruct((OB_DEV, BLOCK), j...]
    ppermute x12, waiting for transfers between devices: 14.9 us -> 12.2 us  [plane_step(): return lax.ppermute(value, 'zone', pairs)]
  transfers between devices with their start and end apart: 24 -> 24, of which waited for: 16 -> 16; matrix products, arithmetic and copies ran while one was open for 1% -> 1% of each run, Pallas kernels for 5% -> 11%
where the time goes in v1:
time: 234 us; the launch traced here: 232 us
  Pallas kernels  106 us (45%)
  starting transfers between devices  91.1 us (39%)
  waiting for transfers between devices  26.4 us (11%)
  other arithmetic  3.85 us (2%)
  local copies, waits for them, and re-layouts  3.32 us (1%)
    pallas_call x3, Pallas kernels, half_sweep(): pl.pallas_call(kernel, out_shape=jax.ShapeDtypeStruct((kept_blocks, BLOCK...  63.2 us
    pallas_call x2, Pallas kernels, first_half_sweep(): pl.pallas_call(kernel, out_shape=(jax.ShapeDtypeStruct((OB_DEV, BLOCK), j...  31.6 us
    ppermute x12, starting transfers between devices, plane_step(): return lax.ppermute(value, 'zone', pairs)  30.1 us
    ppermute x6, starting transfers between devices, along_z(): lax.ppermute(value, 'sub', [(i, (i + step) % SUBS) for i in range(SUBS)])  27 us
    all_to_all x1, starting transfers between devices, shards(): parts = lax.all_to_all(partial, 'zone', 0, 0, tiled=True)  25.7 us
    ppermute x12, waiting for transfers between devices, plane_step(): return lax.ppermute(value, 'zone', pairs)  12.2 us
    ppermute x5, starting transfers between devices, other_core(): lax.ppermute(value, 'zone', [(zone_of(y, x, c), zone_of(y, x, 1 - c)) for...  8.28 us
    all_to_all x1, waiting for transfers between devices, shards(): parts = lax.all_to_all(partial, 'zone', 0, 0, tiled=True)  6.7 us
  transfers between devices with their start and end apart: 24, of which 16 were waited for; matrix products, arithmetic and copies ran while one was open for 1% of the time, Pallas kernels for 11%

profile of v1, /device:TPU:1, one launch (start us, length us, event | category | flops | bytes accessed | tf_op | source)
XLA Modules:
  0.0 232.4 jit_solution(13998317658661741564)
XLA Ops:
  3.8 2.2 collective-permute-start
  6.0 2.6 %collective-permute-start.1 = (bf16[528,128]{1,0:T(8,128)(2,1)S(1)}, bf16[528,128]{1,0:T(8,128)(2,1)S(1)}, u32[]{:S(2)}, u32[]{:S(2)}) collective-permute-start(bf16[528,128]{1,0:T(8,128)(2,1)S(1)} %pad_maximum_fusion), channel_id=1, source_target_pairs={{0,16},{4,68},{8,24},{12,76},{16,0},{20,84},{24,8},{28,92},{32,48}... | collective-permute-start | bytes 405512 | tf_op jit(solution)/shard_map/ppermute | solution.py:54
  10.2 2.6 %collective-permute-done.1 = bf16[528,128]{1,0:T(8,128)(2,1)S(1)} collective-permute-done((bf16[528,128]{1,0:T(8,128)(2,1)S(1)}, bf16[528,128]{1,0:T(8,128)(2,1)S(1)}, u32[]{:S(2)}, u32[]{:S(2)}) %collective-permute-start.1) | collective-permute-done | bytes 135200 | tf_op jit(solution)/shard_map/ppermute | solution.py:54
  12.8 1.9 collective-permute-start.6
  14.7 2.4 %collective-permute-start.5 = (bf16[2112,128]{1,0:T(8,128)(2,1)S(1)}, bf16[2112,128]{1,0:T(8,128)(2,1)S(1)}, u32[]{:S(2)}, u32[]{:S(2)}) collective-permute-start(bf16[2112,128]{1,0:T(8,128)(2,1)S(1)} %constant_dynamic-update-slice_fusion.refs_4_), channel_id=1, source_target_pairs={{0,96},{4,28},{8,104},{12,4},{16,112},{20,12},{24,120},{28,20},{32... | collective-permute-start | bytes 1622024 | tf_op jit(solution)/shard_map/ppermute | solution.py:54
  19.4 2.7 %first_lists.1 = (s32[272]{0:T(512)S(1)}, s32[272]{0:T(512)S(1)}, s32[1]{0:T(128)}, s32[1]{0:T(128)}, s32[32]{0:T(128)S(1)}) custom-call(s32[128]{0:T(128)S(1)} %get-tuple-element.46.pair_ref), custom_call_target="tpu_custom_call" | custom-call | tf_op jit(solution)/shard_map/first_lists/pallas_call | solution.py:208
  22.0 6.6 %embed_orders.1.refs_8_.refs_12_.refs_2_.refs_3_ = bf16[8192,128]{1,0:T(8,128)(2,1)S(1)} custom-call(bf16[8192,128]{1,0:T(8,128)(2,1)} %x_hbm.1, bf16[128,512]{1,0:T(8,128)(2,1)} %w_in_hbm.1, f32[1,512]{1,0:T(1,128)} %bitcast.22, bf16[512,128]{1,0:T(8,128)(2,1)} %w_out_hbm.1, f32[1,128]{1,0:T(1,128)} %bitcast.23), custom_call_target="tpu_custom_call" | custom-call | flops 2147483648 | bytes 4194304 | tf_op jit(solution)/shard_map/embed_orders/pallas_call | solution.py:142
  30.7 14.5 %orders_1_early.1 = f32[16,512]{1,0:T(8,128)S(1)} custom-call(s32[272]{0:T(512)S(1)} %get-tuple-element.28.refs_0_, s32[1]{0:T(128)} %get-tuple-element.29.refs_1_, s32[1]{0:T(128)} %bitcast.2.refs_2_, s32[32]{0:T(128)S(1)} %get-tuple-element.26.refs_3_, bf16[2112,128]{1,0:T(8,128)(2,1)S(1)} %constant_dynamic-update-slice_fusion.refs_4_, ...), custom_call_target="tpu_custom_call" | custom-call | flops 939524096 | bytes 6291456 | tf_op jit(solution)/shard_map/orders_1_early/pallas_call | solution.py:416
  47.2 17.1 %orders_1.1 = (f32[16,512]{1,0:T(8,128)S(1)}, bf16[16896,128]{1,0:T(8,128)(2,1)S(1)}, f32[32,512]{1,0:T(8,128)S(1)}) custom-call(s32[272]{0:T(512)S(1)} %get-tuple-element.24.refs_0_, s32[1]{0:T(128)} %get-tuple-element.25.refs_1_, s32[1]{0:T(128)} %bitcast.2.refs_2_, s32[32]{0:T(128)S(1)} %get-tuple-element.26.refs_3_, ...), custom_call_target="tpu_custom_call" | custom-call | flops 939524096 | bytes 6291456 | tf_op jit(solution)/shard_map/orders_1/pallas_call | solution.py:416
  64.4 9.0 %collective-permute-start.12 = (f32[16,512]{1,0:T(8,128)S(1)}, f32[16,512]{1,0:T(8,128)S(1)}, u32[]{:S(2)}, u32[]{:S(2)}) collective-permute-start(f32[16,512]{1,0:T(8,128)S(1)} %multiply_add_fusion.2), channel_id=1, source_target_pairs={{0,3},{1,0},{2,1},{3,2},{4,7},{5,4},{6,5},{7,6},{8,11},{9,8},{10,9... | collective-permute-start | bytes 98312 | tf_op jit(solution)/shard_map/ppermute | solution.py:46
  74.4 2.2 work_list.1
  78.0 21.1 %couriers_1.1 = f32[32,512]{1,0:T(8,128)S(1)} custom-call(s32[272]{0:T(512)S(1)} %get-tuple-element.37.refs_0_, s32[1]{0:T(128)} %get-tuple-element.38.refs_1_, bf16[8192,128]{1,0:T(8,128)(2,1)S(1)} %embed_orders.1.refs_8_.refs_12_.refs_2_.refs_3_, bf16[16896,128]{1,0:T(8,128)(2,1)S(1)} %get-tuple-element.39.refs_3_.refs_2_, ...), custom_call_target="tpu_custom_call" | custom-call | flops 1879048192 | bytes 6291456 | tf_op jit(solution)/shard_map/couriers_1/pallas_call | solution.py:349
  99.1 4.4 %collective-permute-start.13 = (f32[32,512]{1,0:T(8,128)S(1)}, f32[32,512]{1,0:T(8,128)S(1)}, u32[]{:S(2)}, u32[]{:S(2)}) collective-permute-start(f32[32,512]{1,0:T(8,128)S(1)} %couriers_1.1), channel_id=1, source_target_pairs={{0,4},{4,0},{8,12},{12,8},{16,20},{20,16},{24,28},{28,24},{32,36},... | collective-permute-start | bytes 196616 | tf_op jit(solution)/shard_map/ppermute | solution.py:42
  104.4 15.3 %collective-permute-start.16 = (f32[32,512]{1,0:T(8,128)S(1)}, f32[32,512]{1,0:T(8,128)S(1)}, u32[]{:S(2)}, u32[]{:S(2)}) collective-permute-start(f32[32,512]{1,0:T(8,128)S(1)} %multiply_add_fusion.1), channel_id=1, source_target_pairs={{0,24},{4,100},{8,0},{12,108},{16,8},{20,116},{24,16},{28,124},{32... | collective-permute-start | bytes 196616 | tf_op jit(solution)/shard_map/ppermute | solution.py:54
  121.6 2.8 %collective-permute-done.15 = f32[32,512]{1,0:T(8,128)S(1)} collective-permute-done((f32[32,512]{1,0:T(8,128)S(1)}, f32[32,512]{1,0:T(8,128)S(1)}, u32[]{:S(2)}, u32[]{:S(2)}) %collective-permute-start.15) | collective-permute-done | bytes 65568 | tf_op jit(solution)/shard_map/ppermute | solution.py:54
  124.8 4.7 %collective-permute-start.19 = (f32[32,512]{1,0:T(8,128)S(1)}, f32[32,512]{1,0:T(8,128)S(1)}, u32[]{:S(2)}, u32[]{:S(2)}) collective-permute-start(f32[32,512]{1,0:T(8,128)S(1)} %multiply_add_fusion), channel_id=1, source_target_pairs={{0,96},{4,28},{8,104},{12,4},{16,112},{20,12},{24,120},{28,20},{32... | collective-permute-start | bytes 196616 | tf_op jit(solution)/shard_map/ppermute | solution.py:54
  131.4 2.8 %collective-permute-done.18 = f32[32,512]{1,0:T(8,128)S(1)} collective-permute-done((f32[32,512]{1,0:T(8,128)S(1)}, f32[32,512]{1,0:T(8,128)S(1)}, u32[]{:S(2)}, u32[]{:S(2)}) %collective-permute-start.18) | collective-permute-done | bytes 65568 | tf_op jit(solution)/shard_map/ppermute | solution.py:54
  134.6 21.0 %orders_2.1 = f32[16,512]{1,0:T(8,128)S(1)} custom-call(s32[272]{0:T(512)S(1)} %get-tuple-element.37.refs_0_, s32[1]{0:T(128)} %get-tuple-element.38.refs_1_, bf16[16896,128]{1,0:T(8,128)(2,1)S(1)} %get-tuple-element.39.refs_3_.refs_2_, bf16[8192,128]{1,0:T(8,128)(2,1)S(1)} %embed_orders.1.refs_8_.refs_12_.refs_2_.refs_3_, ...), custom_call_target="tpu_custom_call" | custom-call | flops 1879048192 | bytes 6291456 | tf_op jit(solution)/shard_map/orders_2/pallas_call | solution.py:349
  155.6 4.8 %collective-permute-start.22 = (f32[16,512]{1,0:T(8,128)S(1)}, f32[16,512]{1,0:T(8,128)S(1)}, u32[]{:S(2)}, u32[]{:S(2)}) collective-permute-start(f32[16,512]{1,0:T(8,128)S(1)} %orders_2.1), channel_id=1, source_target_pairs={{0,3},{1,0},{2,1},{3,2},{4,7},{5,4},{6,5},{7,6},{8,11},{9,8},{10,9... | collective-permute-start | bytes 98312 | tf_op jit(solution)/shard_map/ppermute | solution.py:46
  160.4 12.4 %collective-permute-start.21 = (f32[16,512]{1,0:T(8,128)S(1)}, f32[16,512]{1,0:T(8,128)S(1)}, u32[]{:S(2)}, u32[]{:S(2)}) collective-permute-start(f32[16,512]{1,0:T(8,128)S(1)} %orders_2.1), channel_id=1, source_target_pairs={{0,2},{1,3},{2,0},{3,1},{4,6},{5,7},{6,4},{7,5},{8,10},{9,11},{10,... | collective-permute-start | bytes 98312 | tf_op jit(solution)/shard_map/ppermute | solution.py:46
  174.0 2.7 %collective-permute-done.20 = f32[16,512]{1,0:T(8,128)S(1)} collective-permute-done((f32[16,512]{1,0:T(8,128)S(1)}, f32[16,512]{1,0:T(8,128)S(1)}, u32[]{:S(2)}, u32[]{:S(2)}) %collective-permute-start.20) | collective-permute-done | bytes 32800 | tf_op jit(solution)/shard_map/ppermute | solution.py:46
  176.8 21.1 %couriers_2.1 = f32[32,512]{1,0:T(8,128)S(1)} custom-call(s32[272]{0:T(512)S(1)} %get-tuple-element.37.refs_0_, s32[1]{0:T(128)} %get-tuple-element.38.refs_1_, bf16[8192,128]{1,0:T(8,128)(2,1)S(1)} %embed_orders.1.refs_8_.refs_12_.refs_2_.refs_3_, bf16[16896,128]{1,0:T(8,128)(2,1)S(1)} %get-tuple-element.39.refs_3_.refs_2_, ...), custom_call_target="tpu_custom_call" | custom-call | flops 1879048192 | bytes 6291456 | tf_op jit(solution)/shard_map/couriers_2/pallas_call | solution.py:349
  198.6 25.7 %all-to-all-start = ((f32[32,1,512]{2,1,0:T(1,128)}), f32[32,1,512]{2,1,0:T(1,128)S(1)}, u32[]{:S(2)}, u32[]{:S(2)}) async-start(f32[32,1,512]{2,1,0:T(1,128)} %copy.17), calls=%async_computation | async-start | bytes 131072 | tf_op jit(solution)/shard_map/all_to_all | solution.py:497
  225.0 6.7 %all-to-all-done = f32[32,1,512]{2,1,0:T(1,128)S(1)} async-done(((f32[32,1,512]{2,1,0:T(1,128)}), f32[32,1,512]{2,1,0:T(1,128)S(1)}, u32[]{:S(2)}, u32[]{:S(2)}) %all-to-all-start) | async-done | bytes 65568 | tf_op jit(solution)/shard_map/all_to_all | solution.py:497
  (69 shorter events, 21.8 us)
Async XLA Ops:
  3.8 6.3 %collective-permute-start = (bf16[528,128]{1,0:T(8,128)(2,1)S(1)}, bf16[528,128]{1,0:T(8,128)(2,1)S(1)}, u32[]{:S(2)}, u32[]{:S(2)}) collective-permute-start(bf16[528,128]{1,0:T(8,128)(2,1)S(1)} %pad_maximum_fusion), channel_id=1, source_target_pairs={{0,8},{4,36},{8,16},{12,44},{16,24},{20,52},{24,0},{28,60},{32,40}... | collective-permute-start | bytes 405512 | tf_op jit(solution)/shard_map/ppermute | solution.py:54
  6.0 6.8 %collective-permute-start.1 = (bf16[528,128]{1,0:T(8,128)(2,1)S(1)}, bf16[528,128]{1,0:T(8,128)(2,1)S(1)}, u32[]{:S(2)}, u32[]{:S(2)}) collective-permute-start(bf16[528,128]{1,0:T(8,128)(2,1)S(1)} %pad_maximum_fusion), channel_id=1, source_target_pairs={{0,16},{4,68},{8,24},{12,76},{16,0},{20,84},{24,8},{28,92},{32,48}... | collective-permute-start | bytes 405512 | tf_op jit(solution)/shard_map/ppermute | solution.py:54
  8.6 4.2 %collective-permute-start.2 = (bf16[528,128]{1,0:T(8,128)(2,1)S(1)}, bf16[528,128]{1,0:T(8,128)(2,1)S(1)}, u32[]{:S(2)}, u32[]{:S(2)}) collective-permute-start(bf16[528,128]{1,0:T(8,128)(2,1)S(1)} %pad_maximum_fusion), channel_id=1, source_target_pairs={{0,24},{4,100},{8,0},{12,108},{16,8},{20,116},{24,16},{28,124},{32... | collective-permute-start | bytes 405512 | tf_op jit(solution)/shard_map/ppermute | solution.py:54
  12.8 17.9 %collective-permute-start.6 = (bf16[2112,128]{1,0:T(8,128)(2,1)S(1)}, bf16[2112,128]{1,0:T(8,128)(2,1)S(1)}, u32[]{:S(2)}, u32[]{:S(2)}) collective-permute-start(bf16[2112,128]{1,0:T(8,128)(2,1)S(1)} %constant_dynamic-update-slice_fusion.refs_4_), channel_id=1, source_target_pairs={{0,4},{4,0},{8,12},{12,8},{16,20},{20,16},{24,28},{28,24},{32,36},... | collective-permute-start | bytes 1622024 | tf_op jit(solution)/shard_map/ppermute | solution.py:42
  14.7 14.5 %collective-permute-start.5 = (bf16[2112,128]{1,0:T(8,128)(2,1)S(1)}, bf16[2112,128]{1,0:T(8,128)(2,1)S(1)}, u32[]{:S(2)}, u32[]{:S(2)}) collective-permute-start(bf16[2112,128]{1,0:T(8,128)(2,1)S(1)} %constant_dynamic-update-slice_fusion.refs_4_), channel_id=1, source_target_pairs={{0,96},{4,28},{8,104},{12,4},{16,112},{20,12},{24,120},{28,20},{32... | collective-permute-start | bytes 1622024 | tf_op jit(solution)/shard_map/ppermute | solution.py:54
  17.1 12.1 %collective-permute-start.4 = (bf16[2112,128]{1,0:T(8,128)(2,1)S(1)}, bf16[2112,128]{1,0:T(8,128)(2,1)S(1)}, u32[]{:S(2)}, u32[]{:S(2)}) collective-permute-start(bf16[2112,128]{1,0:T(8,128)(2,1)S(1)} %constant_dynamic-update-slice_fusion.refs_4_), channel_id=1, source_target_pairs={{0,64},{4,20},{8,72},{12,28},{16,80},{20,4},{24,88},{28,12},{32,96... | collective-permute-start | bytes 1622024 | tf_op jit(solution)/shard_map/ppermute | solution.py:54
  17.5 27.7 %collective-permute-start.3 = (bf16[2112,128]{1,0:T(8,128)(2,1)S(1)}, bf16[2112,128]{1,0:T(8,128)(2,1)S(1)}, u32[]{:S(2)}, u32[]{:S(2)}) collective-permute-start(bf16[2112,128]{1,0:T(8,128)(2,1)S(1)} %constant_dynamic-update-slice_fusion.refs_4_), channel_id=1, source_target_pairs={{0,32},{4,12},{8,40},{12,20},{16,48},{20,28},{24,56},{28,4},{32,64... | collective-permute-start | bytes 1622024 | tf_op jit(solution)/shard_map/ppermute | solution.py:54
  29.2 18.1 %collective-permute-start.8 = (bf16[2112,128]{1,0:T(8,128)(2,1)S(1)}, bf16[2112,128]{1,0:T(8,128)(2,1)S(1)}, u32[]{:S(2)}, u32[]{:S(2)}) collective-permute-start(bf16[2112,128]{1,0:T(8,128)(2,1)S(1)} %collective-permute-done.4.refs_5_.refs_6_), channel_id=1, source_target_pairs={{0,4},{4,0},{8,12},{12,8},{16,20},{20,16},{24,28},{28,24},{32,36},... | collective-permute-start | bytes 1622024 | tf_op jit(solution)/shard_map/ppermute | solution.py:42
  30.6 16.6 %collective-permute-start.9 = (bf16[2112,128]{1,0:T(8,128)(2,1)S(1)}, bf16[2112,128]{1,0:T(8,128)(2,1)S(1)}, u32[]{:S(2)}, u32[]{:S(2)}) collective-permute-start(bf16[2112,128]{1,0:T(8,128)(2,1)S(1)} %collective-permute-done.5.refs_6_.refs_7_), channel_id=1, source_target_pairs={{0,4},{4,0},{8,12},{12,8},{16,20},{20,16},{24,28},{28,24},{32,36},... | collective-permute-start | bytes 1622024 | tf_op jit(solution)/shard_map/ppermute | solution.py:42
  45.2 2.1 collective-permute-start.7
  64.4 12.2 %collective-permute-start.12 = (f32[16,512]{1,0:T(8,128)S(1)}, f32[16,512]{1,0:T(8,128)S(1)}, u32[]{:S(2)}, u32[]{:S(2)}) collective-permute-start(f32[16,512]{1,0:T(8,128)S(1)} %multiply_add_fusion.2), channel_id=1, source_target_pairs={{0,3},{1,0},{2,1},{3,2},{4,7},{5,4},{6,5},{7,6},{8,11},{9,8},{10,9... | collective-permute-start | bytes 98312 | tf_op jit(solution)/shard_map/ppermute | solution.py:46
  73.4 4.4 %collective-permute-start.11 = (f32[16,512]{1,0:T(8,128)S(1)}, f32[16,512]{1,0:T(8,128)S(1)}, u32[]{:S(2)}, u32[]{:S(2)}) collective-permute-start(f32[16,512]{1,0:T(8,128)S(1)} %multiply_add_fusion.2), channel_id=1, source_target_pairs={{0,2},{1,3},{2,0},{3,1},{4,6},{5,7},{6,4},{7,5},{8,10},{9,11},{10,... | collective-permute-start | bytes 98312 | tf_op jit(solution)/shard_map/ppermute | solution.py:46
  73.6 4.3 %collective-permute-start.10 = (f32[16,512]{1,0:T(8,128)S(1)}, f32[16,512]{1,0:T(8,128)S(1)}, u32[]{:S(2)}, u32[]{:S(2)}) collective-permute-start(f32[16,512]{1,0:T(8,128)S(1)} %multiply_add_fusion.2), channel_id=1, source_target_pairs={{0,1},{1,2},{2,3},{3,0},{4,5},{5,6},{6,7},{7,4},{8,9},{9,10},{10,1... | collective-permute-start | bytes 98312 | tf_op jit(solution)/shard_map/ppermute | solution.py:46
  99.1 5.3 %collective-permute-start.13 = (f32[32,512]{1,0:T(8,128)S(1)}, f32[32,512]{1,0:T(8,128)S(1)}, u32[]{:S(2)}, u32[]{:S(2)}) collective-permute-start(f32[32,512]{1,0:T(8,128)S(1)} %couriers_1.1), channel_id=1, source_target_pairs={{0,4},{4,0},{8,12},{12,8},{16,20},{20,16},{24,28},{28,24},{32,36},... | collective-permute-start | bytes 196616 | tf_op jit(solution)/shard_map/ppermute | solution.py:42
  104.4 17.2 %collective-permute-start.16 = (f32[32,512]{1,0:T(8,128)S(1)}, f32[32,512]{1,0:T(8,128)S(1)}, u32[]{:S(2)}, u32[]{:S(2)}) collective-permute-start(f32[32,512]{1,0:T(8,128)S(1)} %multiply_add_fusion.1), channel_id=1, source_target_pairs={{0,24},{4,100},{8,0},{12,108},{16,8},{20,116},{24,16},{28,124},{32... | collective-permute-start | bytes 196616 | tf_op jit(solution)/shard_map/ppermute | solution.py:54
  119.7 4.7 %collective-permute-start.15 = (f32[32,512]{1,0:T(8,128)S(1)}, f32[32,512]{1,0:T(8,128)S(1)}, u32[]{:S(2)}, u32[]{:S(2)}) collective-permute-start(f32[32,512]{1,0:T(8,128)S(1)} %multiply_add_fusion.1), channel_id=1, source_target_pairs={{0,16},{4,68},{8,24},{12,76},{16,0},{20,84},{24,8},{28,92},{32,48}... | collective-permute-start | bytes 196616 | tf_op jit(solution)/shard_map/ppermute | solution.py:54
  119.7 5.0 %collective-permute-start.14 = (f32[32,512]{1,0:T(8,128)S(1)}, f32[32,512]{1,0:T(8,128)S(1)}, u32[]{:S(2)}, u32[]{:S(2)}) collective-permute-start(f32[32,512]{1,0:T(8,128)S(1)} %multiply_add_fusion.1), channel_id=1, source_target_pairs={{0,8},{4,36},{8,16},{12,44},{16,24},{20,52},{24,0},{28,60},{32,40}... | collective-permute-start | bytes 196616 | tf_op jit(solution)/shard_map/ppermute | solution.py:54
  124.8 6.6 %collective-permute-start.19 = (f32[32,512]{1,0:T(8,128)S(1)}, f32[32,512]{1,0:T(8,128)S(1)}, u32[]{:S(2)}, u32[]{:S(2)}) collective-permute-start(f32[32,512]{1,0:T(8,128)S(1)} %multiply_add_fusion), channel_id=1, source_target_pairs={{0,96},{4,28},{8,104},{12,4},{16,112},{20,12},{24,120},{28,20},{32... | collective-permute-start | bytes 196616 | tf_op jit(solution)/shard_map/ppermute | solution.py:54
  129.5 4.7 %collective-permute-start.18 = (f32[32,512]{1,0:T(8,128)S(1)}, f32[32,512]{1,0:T(8,128)S(1)}, u32[]{:S(2)}, u32[]{:S(2)}) collective-permute-start(f32[32,512]{1,0:T(8,128)S(1)} %multiply_add_fusion), channel_id=1, source_target_pairs={{0,64},{4,20},{8,72},{12,28},{16,80},{20,4},{24,88},{28,12},{32,96... | collective-permute-start | bytes 196616 | tf_op jit(solution)/shard_map/ppermute | solution.py:54
  129.5 5.0 %collective-permute-start.17 = (f32[32,512]{1,0:T(8,128)S(1)}, f32[32,512]{1,0:T(8,128)S(1)}, u32[]{:S(2)}, u32[]{:S(2)}) collective-permute-start(f32[32,512]{1,0:T(8,128)S(1)} %multiply_add_fusion), channel_id=1, source_target_pairs={{0,32},{4,12},{8,40},{12,20},{16,48},{20,28},{24,56},{28,4},{32,64... | collective-permute-start | bytes 196616 | tf_op jit(solution)/shard_map/ppermute | solution.py:54
  155.6 17.1 %collective-permute-start.22 = (f32[16,512]{1,0:T(8,128)S(1)}, f32[16,512]{1,0:T(8,128)S(1)}, u32[]{:S(2)}, u32[]{:S(2)}) collective-permute-start(f32[16,512]{1,0:T(8,128)S(1)} %orders_2.1), channel_id=1, source_target_pairs={{0,3},{1,0},{2,1},{3,2},{4,7},{5,4},{6,5},{7,6},{8,11},{9,8},{10,9... | collective-permute-start | bytes 98312 | tf_op jit(solution)/shard_map/ppermute | solution.py:46
  160.4 13.7 %collective-permute-start.21 = (f32[16,512]{1,0:T(8,128)S(1)}, f32[16,512]{1,0:T(8,128)S(1)}, u32[]{:S(2)}, u32[]{:S(2)}) collective-permute-start(f32[16,512]{1,0:T(8,128)S(1)} %orders_2.1), channel_id=1, source_target_pairs={{0,2},{1,3},{2,0},{3,1},{4,6},{5,7},{6,4},{7,5},{8,10},{9,11},{10,... | collective-permute-start | bytes 98312 | tf_op jit(solution)/shard_map/ppermute | solution.py:46
  172.7 4.0 %collective-permute-start.20 = (f32[16,512]{1,0:T(8,128)S(1)}, f32[16,512]{1,0:T(8,128)S(1)}, u32[]{:S(2)}, u32[]{:S(2)}) collective-permute-start(f32[16,512]{1,0:T(8,128)S(1)} %orders_2.1), channel_id=1, source_target_pairs={{0,1},{1,2},{2,3},{3,0},{4,5},{5,6},{6,7},{7,4},{8,9},{9,10},{10,1... | collective-permute-start | bytes 98312 | tf_op jit(solution)/shard_map/ppermute | solution.py:46
  198.6 33.0 %all-to-all-start = ((f32[32,1,512]{2,1,0:T(1,128)}), f32[32,1,512]{2,1,0:T(1,128)S(1)}, u32[]{:S(2)}, u32[]{:S(2)}) async-start(f32[32,1,512]{2,1,0:T(1,128)} %copy.17), calls=%async_computation | async-start | bytes 131072 | tf_op jit(solution)/shard_map/all_to_all | solution.py:497
  (3 other events, 76.6 us)

commit v2 on v0

--- a/solution.py
+++ b/solution.py
@@ -55,8 +55,41 @@
     return lax.ppermute(value, "zone", pairs)
 
 
-def gather_row(block):
-    return jnp.concatenate([block] + [plane_step(block, 0, step) for step in (1, 2, 3)], axis=0)
+def pack_kernel(count_ref, embed_ref, cap_ref, block_ref, row_ref, sem):
+    copy = pltpu.make_async_copy(embed_ref, block_ref.at[pl.ds(0, BLOCK), :], sem.at[0])
+    copy_row = pltpu.make_async_copy(embed_ref, row_ref.at[pl.ds(0, BLOCK), :], sem.at[1])
+    copy.start()
+    copy_row.start()
+    lane = lax.broadcasted_iota(jnp.int32, (1, BLOCK), 1)
+    cap = jnp.where(lane < count_ref[0], cap_ref[...].astype(jnp.float32), 0.0)
+    rows = [cap[:, i * EMB : (i + 1) * EMB] for i in range(4)]
+    tail = jnp.concatenate(rows + [jnp.zeros((12, EMB), jnp.float32)], axis=0).astype(jnp.bfloat16)
+    block_ref[pl.ds(BLOCK, 16), :] = tail
+    row_ref[pl.ds(BLOCK, 16), :] = tail
+    copy.wait()
+    copy_row.wait()
+
+
+def pack(count, embed, cap):
+    vmem = pl.BlockSpec(memory_space=pltpu.VMEM)
+    return pl.pallas_call(
+        pack_kernel,
+        out_shape=(
+            jax.ShapeDtypeStruct((COURIER_ROWS, EMB), jnp.bfloat16),
+            jax.ShapeDtypeStruct((4 * COURIER_ROWS, EMB), jnp.bfloat16),
+        ),
+        in_specs=[pl.BlockSpec(memory_space=pltpu.SMEM), pl.BlockSpec(memory_space=pltpu.HBM), vmem],
+        out_specs=(vmem, vmem),
+        scratch_shapes=[pltpu.SemaphoreType.DMA((2,))],
+        compiler_params=pltpu.CompilerParams(vmem_limit_bytes=4 * 1024 * 1024),
+        name="pack",
+    )(count, pltpu.with_memory_space_constraint(embed, pltpu.HBM), cap.reshape(1, BLOCK))
+
+
+def gather_row(block, row):
+    for step in (1, 2, 3):
+        row = lax.dynamic_update_slice(row, plane_step(block, 0, step), (step * COURIER_ROWS, 0))
+    return row
 
 
 def gather_plane(row, meanwhile):
@@ -201,6 +234,12 @@
     rounds = rounds_ref[0]
     weight = weight_ref[...]
 
+    def put(cut, value):
+        if len(out_ref.shape) == 3:
+            out_ref[:, 0, cut] = value
+        else:
+            out_ref[:, cut] = value
+
     high = weight.astype(jnp.bfloat16).astype(jnp.float32)
     low = weight - high
     blank = jnp.zeros((64 - 2 * summed_blocks, 128), jnp.float32)
@@ -245,7 +284,7 @@
         for (_, k, _, _), part in zip(todo, sums):
             r_ref[k // 2, k % 2] += part
 
-    large = rounds // (UNROLL // REST)
+    large_steps = rounds // (UNROLL // REST)
 
     def large_step(i, carry):
         steps(i * UNROLL, UNROLL)
@@ -255,18 +294,21 @@
         steps(i * REST, REST)
         return carry
 
-    lax.fori_loop(0, large, large_step, 0)
-    lax.fori_loop(large * (UNROLL // REST), rounds, small_step, 0)
-
-    live_weight = jnp.where(weight > 0.5 * LOWEST, jnp.abs(weight), 0.0)
-    bad = jnp.where(jnp.max(live_weight) <= 128.0, 0.0, 1.0)
+    lax.fori_loop(0, large_steps, large_step, 0)
+    lax.fori_loop(large_steps * (UNROLL // REST), rounds, small_step, 0)
+
+    large = jnp.where((weight > 0.5 * LOWEST) & ~(jnp.abs(weight) <= 128.0), 1.0, 0.0)
+    bad = jnp.max(large, axis=0, keepdims=True)
+    bad = jnp.maximum(bad[:, 0:HALF], bad[:, HALF:])
     for half in range(2):
         cut = slice(half * HALF, (half + 1) * HALF)
         total = jnp.sum(r_ref[0:kept_blocks, half], axis=1)
         live = live_ref[:, cut] > 0.5 * LOWEST
         fine = (total >= 2.0**-86) & (total <= 2.0**126)
-        bad = bad + jnp.max(jnp.where(live, jnp.where(fine, 0.0, 1.0), 0.0))
-        out_ref[:, cut] = jnp.where(live, jnp.log2(jnp.where(live, total, 1.0)), LOWEST)
+        off = jnp.where(live & ~fine, 1.0, 0.0)
+        bad = jnp.maximum(bad, jnp.max(off, axis=0, keepdims=True))
+        put(cut, jnp.where(live, jnp.log2(jnp.where(live, total, 1.0)), LOWEST))
+    bad = jnp.max(bad)
 
     @pl.when(bad > 0.0)
     def _():
@@ -291,10 +333,10 @@
             cut = slice(half * HALF, (half + 1) * HALF)
             live = live_ref[:, cut] > 0.5 * LOWEST
             total = jnp.where(live, r_ref[0:kept_blocks, half, 0, :], 1.0)
-            out_ref[:, cut] = jnp.where(live, m_ref[0:kept_blocks, half, 0, :] + jnp.log2(total), LOWEST)
-
-
-def half_sweep(sum_couriers, work, rounds, summed, kept, weight, live, name):
+            put(cut, jnp.where(live, m_ref[0:kept_blocks, half, 0, :] + jnp.log2(total), LOWEST))
+
+
+def half_sweep(sum_couriers, work, rounds, summed, kept, weight, live, name, apart=False):
     smem = pl.BlockSpec(memory_space=pltpu.SMEM)
     vmem = pl.BlockSpec(memory_space=pltpu.VMEM)
     summed_blocks, kept_blocks = weight.shape[0], live.shape[0]
@@ -304,7 +346,7 @@
 
     return pl.pallas_call(
         kernel,
-        out_shape=jax.ShapeDtypeStruct((kept_blocks, BLOCK), jnp.float32),
+        out_shape=jax.ShapeDtypeStruct((kept_blocks, 1, BLOCK) if apart else (kept_blocks, BLOCK), jnp.float32),
         in_specs=[smem, smem] + [vmem] * 4,
         out_specs=vmem,
         scratch_shapes=pass_scratch(kept_blocks),
@@ -385,11 +427,10 @@
     positions = jnp.arange(BLOCK, dtype=jnp.int32)
 
     own_live = positions < courier_count[0]
-    tail = jnp.where(own_live, courier_cap, 0).reshape(4, EMB)
-    block = jnp.concatenate([courier_embed, jnp.pad(tail, ((0, 12), (0, 0)))], axis=0)
-    row = gather_row(block)
+    row = gather_row(*pack(courier_count, courier_embed, courier_cap))
     row, bias_in, adjacency, order_count = lax.optimization_barrier((row, bias_in, adjacency, order_count))
     orders = embed_orders(order_features, w_in, bias_in, w_out, bias_out)
+
     parts, orders = gather_plane(row, orders)
 
     mine = adjacency % SUBS == sub
@@ -410,15 +451,15 @@
     )
     courier_here = jnp.where(courier_live & named, 0.0, LOWEST)
 
-    def courier_pass(order_dual, name):
-        return half_sweep(False, work, rounds, orders, couriers, order_dual, courier_here, name)
+    def courier_pass(order_dual, name, apart=False):
+        return half_sweep(False, work, rounds, orders, couriers, order_dual, courier_here, name, apart)
 
     order_dual = order_dual_of(partial)
     sums = join_zones(courier_pass(order_dual, "couriers_1"))
     courier_dual = jnp.where(courier_live, log_cap - sums, LOWEST)
     order_dual = order_dual_of(half_sweep(True, work, rounds, couriers, orders, courier_dual, order_here, "orders_2"))
-    partial = courier_pass(order_dual, "couriers_2")
-    parts = lax.all_to_all(partial, "zone", 0, 0, tiled=True)
+    partial = courier_pass(order_dual, "couriers_2", apart=True)
+    parts = lax.all_to_all(partial, "zone", 0, 0, tiled=True)[:, 0]
     highest = jnp.max(parts, axis=0)
     total = highest + jnp.log2(jnp.sum(jnp.exp2(parts - highest[None]), axis=0))
     own_log_cap = jnp.log2(courier_cap.astype(jnp.float32))

time: 224 us -> 223 us (level)
  Pallas kernels: 150 us -> 139 us
  starting transfers between devices: 39.3 us -> 49.8 us
    pallas_call x3 -> x4, Pallas kernels: 100 us -> 88.6 us  [the longest x3 87.6 us: half_sweep(): pl.pallas_call(kernel, out_shape=jax.ShapeDtypeStruct((kept_blocks, 1, BL...]
    ppermute x6, starting transfers between devices: 7.98 us -> 18.2 us  [along_z(): lax.ppermute(value, 'sub', [(i, (i + step) % SUBS) for i in range(SUBS)])]
  transfers between devices with their start and end apart: 24 -> 24, of which waited for: 16 -> 14; matrix products, arithmetic and copies ran while one was open for 1% -> 1% of each run, Pallas kernels for 5% -> 5%
where the time goes in v2:
time: 223 us
  Pallas kernels  139 us (62%)
  starting transfers between devices  49.8 us (22%)
  waiting for transfers between devices  28.2 us (13%)
  local copies, waits for them, and re-layouts  2.39 us (1%)
    pallas_call x3, Pallas kernels, half_sweep(): pl.pallas_call(kernel, out_shape=jax.ShapeDtypeStruct((kept_blocks, 1, BL...  87.6 us
    pallas_call x1, Pallas kernels, first_half_sweep(): pl.pallas_call(first_kernel, out_shape=(jax.ShapeDtypeStruct((OB_DEV, BLO...  39.2 us
    ppermute x6, starting transfers between devices, along_z(): lax.ppermute(value, 'sub', [(i, (i + step) % SUBS) for i in range(SUBS)])  18.2 us
    ppermute x12, starting transfers between devices, plane_step(): return lax.ppermute(value, 'zone', pairs)  17 us
    ppermute x12, waiting for transfers between devices, plane_step(): return lax.ppermute(value, 'zone', pairs)  15.2 us
    all_to_all x1, starting transfers between devices, shards(): parts = lax.all_to_all(partial, 'zone', 0, 0, tiled=True)[:, 0]  7.9 us
    all_to_all x1, waiting for transfers between devices, shards(): parts = lax.all_to_all(partial, 'zone', 0, 0, tiled=True)[:, 0]  6.7 us
    ppermute x5, starting transfers between devices, other_core(): lax.ppermute(value, 'zone', [(zone_of(y, x, c), zone_of(y, x, 1 - c)) for...  6.66 us
  transfers between devices with their start and end apart: 24, of which 14 were waited for; matrix products, arithmetic and copies ran while one was open for 1% of the time, Pallas kernels for 5%

profile of v2, /device:TPU:1, one launch (start us, length us, event | category | flops | bytes accessed | tf_op | source)
XLA Modules:
  0.0 222.8 jit_solution(11434713284307847879)
XLA Ops:
  3.0 2.2 collective-permute-start
  5.2 2.6 %collective-permute-start.1 = (bf16[528,128]{1,0:T(8,128)(2,1)S(1)}, bf16[528,128]{1,0:T(8,128)(2,1)S(1)}, u32[]{:S(2)}, u32[]{:S(2)}) collective-permute-start(bf16[528,128]{1,0:T(8,128)(2,1)S(1)} %get-tuple-element.20), channel_id=1, source_target_pairs={{0,16},{4,68},{8,24},{12,76},{16,0},{20,84},{24,8},{28,92},{32,48}... | collective-permute-start | bytes 405512 | tf_op jit(solution)/shard_map/ppermute | solution.py:55
  9.3 2.6 %collective-permute-done.1 = bf16[528,128]{1,0:T(8,128)(2,1)S(1)} collective-permute-done((bf16[528,128]{1,0:T(8,128)(2,1)S(1)}, bf16[528,128]{1,0:T(8,128)(2,1)S(1)}, u32[]{:S(2)}, u32[]{:S(2)}) %collective-permute-start.1) | collective-permute-done | bytes 135200 | tf_op jit(solution)/shard_map/ppermute | solution.py:55
  12.0 2.5 %collective-permute-start.5 = (bf16[2112,128]{1,0:T(8,128)(2,1)S(1)}, bf16[2112,128]{1,0:T(8,128)(2,1)S(1)}, u32[]{:S(2)}, u32[]{:S(2)}) collective-permute-start(bf16[2112,128]{1,0:T(8,128)(2,1)S(1)} %constant_dynamic-update-slice_fusion.refs_0_), channel_id=1, source_target_pairs={{0,96},{4,28},{8,104},{12,4},{16,112},{20,12},{24,120},{28,20},{32... | collective-permute-start | bytes 1622024 | tf_op jit(solution)/shard_map/ppermute | solution.py:55
  15.6 2.8 %collective-permute-start.6 = (bf16[2112,128]{1,0:T(8,128)(2,1)S(1)}, bf16[2112,128]{1,0:T(8,128)(2,1)S(1)}, u32[]{:S(2)}, u32[]{:S(2)}) collective-permute-start(bf16[2112,128]{1,0:T(8,128)(2,1)S(1)} %constant_dynamic-update-slice_fusion.refs_0_), channel_id=1, source_target_pairs={{0,4},{4,0},{8,12},{12,8},{16,20},{20,16},{24,28},{28,24},{32,36},... | collective-permute-start | bytes 1622024 | tf_op jit(solution)/shard_map/ppermute | solution.py:43
  20.2 6.6 %embed_orders.1.refs_8_.refs_2_.refs_3_ = bf16[8192,128]{1,0:T(8,128)(2,1)S(1)} custom-call(bf16[8192,128]{1,0:T(8,128)(2,1)} %x_hbm.1, bf16[128,512]{1,0:T(8,128)(2,1)} %w_in_hbm.1, f32[1,512]{1,0:T(1,128)} %bitcast.17, bf16[512,128]{1,0:T(8,128)(2,1)} %w_out_hbm.1, f32[1,128]{1,0:T(1,128)} %bitcast.18), custom_call_target="tpu_custom_call" | custom-call | flops 2147483648 | bytes 4194304 | tf_op jit(solution)/shard_map/embed_orders/pallas_call | solution.py:172
  26.8 3.5 %collective-permute-done.3.refs_1_ = bf16[2112,128]{1,0:T(8,128)(2,1)S(1)} collective-permute-done((bf16[2112,128]{1,0:T(8,128)(2,1)S(1)}, bf16[2112,128]{1,0:T(8,128)(2,1)S(1)}, u32[]{:S(2)}, u32[]{:S(2)}) %collective-permute-start.3) | collective-permute-done | bytes 540704 | tf_op jit(solution)/shard_map/ppermute | solution.py:55
  30.3 3.2 %collective-permute-start.7 = (bf16[2112,128]{1,0:T(8,128)(2,1)S(1)}, bf16[2112,128]{1,0:T(8,128)(2,1)S(1)}, u32[]{:S(2)}, u32[]{:S(2)}) collective-permute-start(bf16[2112,128]{1,0:T(8,128)(2,1)S(1)} %collective-permute-done.3.refs_1_), channel_id=1, source_target_pairs={{0,4},{4,0},{8,12},{12,8},{16,20},{20,16},{24,28},{28,24},{32,36},... | collective-permute-start | bytes 1622024 | tf_op jit(solution)/shard_map/ppermute | solution.py:43
  34.1 2.2 first_list.1
  36.6 39.2 %orders_1.1 = (f32[16,512]{1,0:T(8,128)S(1)}, bf16[16896,128]{1,0:T(8,128)(2,1)S(1)}, f32[32,512]{1,0:T(8,128)S(1)}) custom-call(s32[272]{0:T(512)S(1)} %get-tuple-element.23.work_ref, s32[1]{0:T(128)} %get-tuple-element.24.rounds_ref, s32[1]{0:T(128)} %bitcast.zone_ref, bf16[2112,128]{1,0:T(8,128)(2,1)S(1)} %constant_dynamic-update-slice_fusion.refs_0_, ...), custom_call_target="tpu_custom_call" | custom-call | flops 1879048192 | bytes 6291456 | tf_op jit(solution)/shard_map/orders_1/pallas_call | solution.py:397
  75.8 3.8 %collective-permute-start.12 = (f32[16,512]{1,0:T(8,128)S(1)}, f32[16,512]{1,0:T(8,128)S(1)}, u32[]{:S(2)}, u32[]{:S(2)}) collective-permute-start(f32[16,512]{1,0:T(8,128)S(1)} %get-tuple-element.35), channel_id=1, source_target_pairs={{0,3},{1,0},{2,1},{3,2},{4,7},{5,4},{6,5},{7,6},{8,11},{9,8},{10,9... | collective-permute-start | bytes 98312 | tf_op jit(solution)/shard_map/ppermute | solution.py:47
  80.5 2.2 work_list.1
  84.1 29.2 %couriers_1.1 = f32[32,512]{1,0:T(8,128)S(1)} custom-call(s32[272]{0:T(512)S(1)} %get-tuple-element.32.refs_0_, s32[1]{0:T(128)} %get-tuple-element.33.refs_1_, bf16[8192,128]{1,0:T(8,128)(2,1)S(1)} %embed_orders.1.refs_8_.refs_2_.refs_3_, bf16[16896,128]{1,0:T(8,128)(2,1)S(1)} %get-tuple-element.34.refs_3_.refs_2_, ...), custom_call_target="tpu_custom_call" | custom-call | flops 1879048192 | bytes 6291456 | tf_op jit(solution)/shard_map/couriers_1/pallas_call | solution.py:347
  114.8 1.4 collective-permute-start.14
  116.2 1.9 collective-permute-done.16
  120.7 5.8 %collective-permute-start.18 = (f32[32,512]{1,0:T(8,128)S(1)}, f32[32,512]{1,0:T(8,128)S(1)}, u32[]{:S(2)}, u32[]{:S(2)}) collective-permute-start(f32[32,512]{1,0:T(8,128)S(1)} %multiply_add_fusion), channel_id=1, source_target_pairs={{0,64},{4,20},{8,72},{12,28},{16,80},{20,4},{24,88},{28,12},{32,96... | collective-permute-start | bytes 196616 | tf_op jit(solution)/shard_map/ppermute | solution.py:55
  126.5 1.6 collective-permute-done.18
  128.2 2.7 %collective-permute-done.17 = f32[32,512]{1,0:T(8,128)S(1)} collective-permute-done((f32[32,512]{1,0:T(8,128)S(1)}, f32[32,512]{1,0:T(8,128)S(1)}, u32[]{:S(2)}, u32[]{:S(2)}) %collective-permute-start.17) | collective-permute-done | bytes 65568 | tf_op jit(solution)/shard_map/ppermute | solution.py:55
  130.9 28.8 %orders_2.1 = f32[16,512]{1,0:T(8,128)S(1)} custom-call(s32[272]{0:T(512)S(1)} %get-tuple-element.32.refs_0_, s32[1]{0:T(128)} %get-tuple-element.33.refs_1_, bf16[16896,128]{1,0:T(8,128)(2,1)S(1)} %get-tuple-element.34.refs_3_.refs_2_, bf16[8192,128]{1,0:T(8,128)(2,1)S(1)} %embed_orders.1.refs_8_.refs_2_.refs_3_, ...), custom_call_target="tpu_custom_call" | custom-call | flops 1879048192 | bytes 6291456 | tf_op jit(solution)/shard_map/orders_2/pallas_call | solution.py:347
  159.7 13.1 %collective-permute-start.22 = (f32[16,512]{1,0:T(8,128)S(1)}, f32[16,512]{1,0:T(8,128)S(1)}, u32[]{:S(2)}, u32[]{:S(2)}) collective-permute-start(f32[16,512]{1,0:T(8,128)S(1)} %orders_2.1), channel_id=1, source_target_pairs={{0,3},{1,0},{2,1},{3,2},{4,7},{5,4},{6,5},{7,6},{8,11},{9,8},{10,9... | collective-permute-start | bytes 98312 | tf_op jit(solution)/shard_map/ppermute | solution.py:47
  173.8 3.3 %collective-permute-done.21 = f32[16,512]{1,0:T(8,128)S(1)} collective-permute-done((f32[16,512]{1,0:T(8,128)S(1)}, f32[16,512]{1,0:T(8,128)S(1)}, u32[]{:S(2)}, u32[]{:S(2)}) %collective-permute-start.21) | collective-permute-done | bytes 32800 | tf_op jit(solution)/shard_map/ppermute | solution.py:47
  177.2 29.7 %couriers_2.1 = f32[32,1,512]{2,1,0:T(1,128)} custom-call(s32[272]{0:T(512)S(1)} %get-tuple-element.32.refs_0_, s32[1]{0:T(128)} %get-tuple-element.33.refs_1_, bf16[8192,128]{1,0:T(8,128)(2,1)S(1)} %embed_orders.1.refs_8_.refs_2_.refs_3_, bf16[16896,128]{1,0:T(8,128)(2,1)S(1)} %get-tuple-element.34.refs_3_.refs_2_, ...), custom_call_target="tpu_custom_call" | custom-call | flops 1879048192 | bytes 6291456 | tf_op jit(solution)/shard_map/couriers_2/pallas_call | solution.py:347
  206.9 7.9 %all-to-all-start = ((f32[32,1,512]{2,1,0:T(1,128)}), f32[32,1,512]{2,1,0:T(1,128)S(1)}, u32[]{:S(2)}, u32[]{:S(2)}) async-start(f32[32,1,512]{2,1,0:T(1,128)} %couriers_2.1), calls=%async_computation | async-start | bytes 131072 | tf_op jit(solution)/shard_map/all_to_all | solution.py:462
  215.4 6.7 %all-to-all-done = f32[32,1,512]{2,1,0:T(1,128)S(1)} async-done(((f32[32,1,512]{2,1,0:T(1,128)}), f32[32,1,512]{2,1,0:T(1,128)S(1)}, u32[]{:S(2)}, u32[]{:S(2)}) %all-to-all-start) | async-done | bytes 65568 | tf_op jit(solution)/shard_map/all_to_all | solution.py:462
  (64 shorter events, 15.8 us)
Async XLA Ops:
  3.0 6.3 %collective-permute-start = (bf16[528,128]{1,0:T(8,128)(2,1)S(1)}, bf16[528,128]{1,0:T(8,128)(2,1)S(1)}, u32[]{:S(2)}, u32[]{:S(2)}) collective-permute-start(bf16[528,128]{1,0:T(8,128)(2,1)S(1)} %get-tuple-element.20), channel_id=1, source_target_pairs={{0,8},{4,36},{8,16},{12,44},{16,24},{20,52},{24,0},{28,60},{32,40}... | collective-permute-start | bytes 405512 | tf_op jit(solution)/shard_map/ppermute | solution.py:55
  5.2 6.8 %collective-permute-start.1 = (bf16[528,128]{1,0:T(8,128)(2,1)S(1)}, bf16[528,128]{1,0:T(8,128)(2,1)S(1)}, u32[]{:S(2)}, u32[]{:S(2)}) collective-permute-start(bf16[528,128]{1,0:T(8,128)(2,1)S(1)} %get-tuple-element.20), channel_id=1, source_target_pairs={{0,16},{4,68},{8,24},{12,76},{16,0},{20,84},{24,8},{28,92},{32,48}... | collective-permute-start | bytes 405512 | tf_op jit(solution)/shard_map/ppermute | solution.py:55
  7.8 4.2 %collective-permute-start.2 = (bf16[528,128]{1,0:T(8,128)(2,1)S(1)}, bf16[528,128]{1,0:T(8,128)(2,1)S(1)}, u32[]{:S(2)}, u32[]{:S(2)}) collective-permute-start(bf16[528,128]{1,0:T(8,128)(2,1)S(1)} %get-tuple-element.20), channel_id=1, source_target_pairs={{0,24},{4,100},{8,0},{12,108},{16,8},{20,116},{24,16},{28,124},{32... | collective-permute-start | bytes 405512 | tf_op jit(solution)/shard_map/ppermute | solution.py:55
  12.0 14.8 %collective-permute-start.5 = (bf16[2112,128]{1,0:T(8,128)(2,1)S(1)}, bf16[2112,128]{1,0:T(8,128)(2,1)S(1)}, u32[]{:S(2)}, u32[]{:S(2)}) collective-permute-start(bf16[2112,128]{1,0:T(8,128)(2,1)S(1)} %constant_dynamic-update-slice_fusion.refs_0_), channel_id=1, source_target_pairs={{0,96},{4,28},{8,104},{12,4},{16,112},{20,12},{24,120},{28,20},{32... | collective-permute-start | bytes 1622024 | tf_op jit(solution)/shard_map/ppermute | solution.py:55
  14.5 12.3 %collective-permute-start.4 = (bf16[2112,128]{1,0:T(8,128)(2,1)S(1)}, bf16[2112,128]{1,0:T(8,128)(2,1)S(1)}, u32[]{:S(2)}, u32[]{:S(2)}) collective-permute-start(bf16[2112,128]{1,0:T(8,128)(2,1)S(1)} %constant_dynamic-update-slice_fusion.refs_0_), channel_id=1, source_target_pairs={{0,64},{4,20},{8,72},{12,28},{16,80},{20,4},{24,88},{28,12},{32,96... | collective-permute-start | bytes 1622024 | tf_op jit(solution)/shard_map/ppermute | solution.py:55
  15.0 15.3 %collective-permute-start.3 = (bf16[2112,128]{1,0:T(8,128)(2,1)S(1)}, bf16[2112,128]{1,0:T(8,128)(2,1)S(1)}, u32[]{:S(2)}, u32[]{:S(2)}) collective-permute-start(bf16[2112,128]{1,0:T(8,128)(2,1)S(1)} %constant_dynamic-update-slice_fusion.refs_0_), channel_id=1, source_target_pairs={{0,32},{4,12},{8,40},{12,20},{16,48},{20,28},{24,56},{28,4},{32,64... | collective-permute-start | bytes 1622024 | tf_op jit(solution)/shard_map/ppermute | solution.py:55
  15.6 20.9 %collective-permute-start.6 = (bf16[2112,128]{1,0:T(8,128)(2,1)S(1)}, bf16[2112,128]{1,0:T(8,128)(2,1)S(1)}, u32[]{:S(2)}, u32[]{:S(2)}) collective-permute-start(bf16[2112,128]{1,0:T(8,128)(2,1)S(1)} %constant_dynamic-update-slice_fusion.refs_0_), channel_id=1, source_target_pairs={{0,4},{4,0},{8,12},{12,8},{16,20},{20,16},{24,28},{28,24},{32,36},... | collective-permute-start | bytes 1622024 | tf_op jit(solution)/shard_map/ppermute | solution.py:43
  30.3 6.2 %collective-permute-start.7 = (bf16[2112,128]{1,0:T(8,128)(2,1)S(1)}, bf16[2112,128]{1,0:T(8,128)(2,1)S(1)}, u32[]{:S(2)}, u32[]{:S(2)}) collective-permute-start(bf16[2112,128]{1,0:T(8,128)(2,1)S(1)} %collective-permute-done.3.refs_1_), channel_id=1, source_target_pairs={{0,4},{4,0},{8,12},{12,8},{16,20},{20,16},{24,28},{28,24},{32,36},... | collective-permute-start | bytes 1622024 | tf_op jit(solution)/shard_map/ppermute | solution.py:43
  33.5 3.0 %collective-permute-start.8 = (bf16[2112,128]{1,0:T(8,128)(2,1)S(1)}, bf16[2112,128]{1,0:T(8,128)(2,1)S(1)}, u32[]{:S(2)}, u32[]{:S(2)}) collective-permute-start(bf16[2112,128]{1,0:T(8,128)(2,1)S(1)} %collective-permute-done.4.refs_2_), channel_id=1, source_target_pairs={{0,4},{4,0},{8,12},{12,8},{16,20},{20,16},{24,28},{28,24},{32,36},... | collective-permute-start | bytes 1622024 | tf_op jit(solution)/shard_map/ppermute | solution.py:43
  33.5 3.1 %collective-permute-start.9 = (bf16[2112,128]{1,0:T(8,128)(2,1)S(1)}, bf16[2112,128]{1,0:T(8,128)(2,1)S(1)}, u32[]{:S(2)}, u32[]{:S(2)}) collective-permute-start(bf16[2112,128]{1,0:T(8,128)(2,1)S(1)} %collective-permute-done.5.refs_3_), channel_id=1, source_target_pairs={{0,4},{4,0},{8,12},{12,8},{16,20},{20,16},{24,28},{28,24},{32,36},... | collective-permute-start | bytes 1622024 | tf_op jit(solution)/shard_map/ppermute | solution.py:43
  75.8 6.9 %collective-permute-start.12 = (f32[16,512]{1,0:T(8,128)S(1)}, f32[16,512]{1,0:T(8,128)S(1)}, u32[]{:S(2)}, u32[]{:S(2)}) collective-permute-start(f32[16,512]{1,0:T(8,128)S(1)} %get-tuple-element.35), channel_id=1, source_target_pairs={{0,3},{1,0},{2,1},{3,2},{4,7},{5,4},{6,5},{7,6},{8,11},{9,8},{10,9... | collective-permute-start | bytes 98312 | tf_op jit(solution)/shard_map/ppermute | solution.py:47
  79.7 4.3 %collective-permute-start.11 = (f32[16,512]{1,0:T(8,128)S(1)}, f32[16,512]{1,0:T(8,128)S(1)}, u32[]{:S(2)}, u32[]{:S(2)}) collective-permute-start(f32[16,512]{1,0:T(8,128)S(1)} %get-tuple-element.35), channel_id=1, source_target_pairs={{0,2},{1,3},{2,0},{3,1},{4,6},{5,7},{6,4},{7,5},{8,10},{9,11},{10,... | collective-permute-start | bytes 98312 | tf_op jit(solution)/shard_map/ppermute | solution.py:47
  79.7 4.3 %collective-permute-start.10 = (f32[16,512]{1,0:T(8,128)S(1)}, f32[16,512]{1,0:T(8,128)S(1)}, u32[]{:S(2)}, u32[]{:S(2)}) collective-permute-start(f32[16,512]{1,0:T(8,128)S(1)} %get-tuple-element.35), channel_id=1, source_target_pairs={{0,1},{1,2},{2,3},{3,0},{4,5},{5,6},{6,7},{7,4},{8,9},{9,10},{10,1... | collective-permute-start | bytes 98312 | tf_op jit(solution)/shard_map/ppermute | solution.py:47
  113.2 1.3 collective-permute-start.13
  114.6 3.5 %collective-permute-start.16 = (f32[32,512]{1,0:T(8,128)S(1)}, f32[32,512]{1,0:T(8,128)S(1)}, u32[]{:S(2)}, u32[]{:S(2)}) collective-permute-start(f32[32,512]{1,0:T(8,128)S(1)} %multiply_add_fusion.1), channel_id=1, source_target_pairs={{0,24},{4,100},{8,0},{12,108},{16,8},{20,116},{24,16},{28,124},{32... | collective-permute-start | bytes 196616 | tf_op jit(solution)/shard_map/ppermute | solution.py:55
  114.7 4.7 %collective-permute-start.15 = (f32[32,512]{1,0:T(8,128)S(1)}, f32[32,512]{1,0:T(8,128)S(1)}, u32[]{:S(2)}, u32[]{:S(2)}) collective-permute-start(f32[32,512]{1,0:T(8,128)S(1)} %multiply_add_fusion.1), channel_id=1, source_target_pairs={{0,16},{4,68},{8,24},{12,76},{16,0},{20,84},{24,8},{28,92},{32,48}... | collective-permute-start | bytes 196616 | tf_op jit(solution)/shard_map/ppermute | solution.py:55
  114.8 5.7 %collective-permute-start.14 = (f32[32,512]{1,0:T(8,128)S(1)}, f32[32,512]{1,0:T(8,128)S(1)}, u32[]{:S(2)}, u32[]{:S(2)}) collective-permute-start(f32[32,512]{1,0:T(8,128)S(1)} %multiply_add_fusion.1), channel_id=1, source_target_pairs={{0,8},{4,36},{8,16},{12,44},{16,24},{20,52},{24,0},{28,60},{32,40}... | collective-permute-start | bytes 196616 | tf_op jit(solution)/shard_map/ppermute | solution.py:55
  120.6 6.0 %collective-permute-start.19 = (f32[32,512]{1,0:T(8,128)S(1)}, f32[32,512]{1,0:T(8,128)S(1)}, u32[]{:S(2)}, u32[]{:S(2)}) collective-permute-start(f32[32,512]{1,0:T(8,128)S(1)} %multiply_add_fusion), channel_id=1, source_target_pairs={{0,96},{4,28},{8,104},{12,4},{16,112},{20,12},{24,120},{28,20},{32... | collective-permute-start | bytes 196616 | tf_op jit(solution)/shard_map/ppermute | solution.py:55
  120.7 7.5 %collective-permute-start.18 = (f32[32,512]{1,0:T(8,128)S(1)}, f32[32,512]{1,0:T(8,128)S(1)}, u32[]{:S(2)}, u32[]{:S(2)}) collective-permute-start(f32[32,512]{1,0:T(8,128)S(1)} %multiply_add_fusion), channel_id=1, source_target_pairs={{0,64},{4,20},{8,72},{12,28},{16,80},{20,4},{24,88},{28,12},{32,96... | collective-permute-start | bytes 196616 | tf_op jit(solution)/shard_map/ppermute | solution.py:55
  126.5 4.3 %collective-permute-start.17 = (f32[32,512]{1,0:T(8,128)S(1)}, f32[32,512]{1,0:T(8,128)S(1)}, u32[]{:S(2)}, u32[]{:S(2)}) collective-permute-start(f32[32,512]{1,0:T(8,128)S(1)} %multiply_add_fusion), channel_id=1, source_target_pairs={{0,32},{4,12},{8,40},{12,20},{16,48},{20,28},{24,56},{28,4},{32,64... | collective-permute-start | bytes 196616 | tf_op jit(solution)/shard_map/ppermute | solution.py:55
  159.7 14.1 %collective-permute-start.22 = (f32[16,512]{1,0:T(8,128)S(1)}, f32[16,512]{1,0:T(8,128)S(1)}, u32[]{:S(2)}, u32[]{:S(2)}) collective-permute-start(f32[16,512]{1,0:T(8,128)S(1)} %orders_2.1), channel_id=1, source_target_pairs={{0,3},{1,0},{2,1},{3,2},{4,7},{5,4},{6,5},{7,6},{8,11},{9,8},{10,9... | collective-permute-start | bytes 98312 | tf_op jit(solution)/shard_map/ppermute | solution.py:47
  172.8 4.3 %collective-permute-start.21 = (f32[16,512]{1,0:T(8,128)S(1)}, f32[16,512]{1,0:T(8,128)S(1)}, u32[]{:S(2)}, u32[]{:S(2)}) collective-permute-start(f32[16,512]{1,0:T(8,128)S(1)} %orders_2.1), channel_id=1, source_target_pairs={{0,2},{1,3},{2,0},{3,1},{4,6},{5,7},{6,4},{7,5},{8,10},{9,11},{10,... | collective-permute-start | bytes 98312 | tf_op jit(solution)/shard_map/ppermute | solution.py:47
  172.8 4.3 %collective-permute-start.20 = (f32[16,512]{1,0:T(8,128)S(1)}, f32[16,512]{1,0:T(8,128)S(1)}, u32[]{:S(2)}, u32[]{:S(2)}) collective-permute-start(f32[16,512]{1,0:T(8,128)S(1)} %orders_2.1), channel_id=1, source_target_pairs={{0,1},{1,2},{2,3},{3,0},{4,5},{5,6},{6,7},{7,4},{8,9},{9,10},{10,1... | collective-permute-start | bytes 98312 | tf_op jit(solution)/shard_map/ppermute | solution.py:47
  206.9 15.2 %all-to-all-start = ((f32[32,1,512]{2,1,0:T(1,128)}), f32[32,1,512]{2,1,0:T(1,128)S(1)}, u32[]{:S(2)}, u32[]{:S(2)}) async-start(f32[32,1,512]{2,1,0:T(1,128)} %couriers_2.1), calls=%async_computation | async-start | bytes 131072 | tf_op jit(solution)/shard_map/all_to_all | solution.py:462
  (3 other events, 77.4 us)

commit v3 on v1

--- a/solution.py
+++ b/solution.py
@@ -54,12 +54,45 @@
     return lax.ppermute(value, "zone", pairs)
 
 
-def gather_row(block):
-    return jnp.concatenate([block] + [plane_step(block, 0, step) for step in (1, 2, 3)], axis=0)
+def pack_kernel(count_ref, embed_ref, cap_ref, block_ref, row_ref, sem):
+    copy = pltpu.make_async_copy(embed_ref, block_ref.at[pl.ds(0, BLOCK), :], sem.at[0])
+    copy_row = pltpu.make_async_copy(embed_ref, row_ref.at[pl.ds(0, BLOCK), :], sem.at[1])
+    copy.start()
+    copy_row.start()
+    lane = lax.broadcasted_iota(jnp.int32, (1, BLOCK), 1)
+    cap = jnp.where(lane < count_ref[0], cap_ref[...].astype(jnp.float32), 0.0)
+    rows = [cap[:, i * EMB : (i + 1) * EMB] for i in range(4)]
+    tail = jnp.concatenate(rows + [jnp.zeros((12, EMB), jnp.float32)], axis=0).astype(jnp.bfloat16)
+    block_ref[pl.ds(BLOCK, 16), :] = tail
+    row_ref[pl.ds(BLOCK, 16), :] = tail
+    copy.wait()
+    copy_row.wait()
+
+
+def pack(count, embed, cap):
+    vmem = pl.BlockSpec(memory_space=pltpu.VMEM)
+    return pl.pallas_call(
+        pack_kernel,
+        out_shape=(
+            jax.ShapeDtypeStruct((COURIER_ROWS, EMB), jnp.bfloat16),
+            jax.ShapeDtypeStruct((4 * COURIER_ROWS, EMB), jnp.bfloat16),
+        ),
+        in_specs=[pl.BlockSpec(memory_space=pltpu.SMEM), pl.BlockSpec(memory_space=pltpu.HBM), vmem],
+        out_specs=(vmem, vmem),
+        scratch_shapes=[pltpu.SemaphoreType.DMA((2,))],
+        compiler_params=pltpu.CompilerParams(vmem_limit_bytes=4 * 1024 * 1024),
+        name="pack",
+    )(count, pltpu.with_memory_space_constraint(embed, pltpu.HBM), cap.reshape(1, BLOCK))
+
+
+def gather_row(block, row):
+    for step in (1, 2, 3):
+        row = lax.dynamic_update_slice(row, plane_step(block, 0, step), (step * COURIER_ROWS, 0))
+    return row
 
 
 PARTS = 8
-EARLY = (0, 2, 3, 4)
+EARLY = (0, 4)
 
 
 def slot_of(zone, me):
@@ -289,7 +322,7 @@
         for (_, k, _, _), part in zip(todo, sums):
             r_ref[k // 2, k % 2] += part
 
-    large = rounds // (UNROLL // REST)
+    large_steps = rounds // (UNROLL // REST)
 
     def large_step(i, carry):
         steps(i * UNROLL, UNROLL)
@@ -299,18 +332,21 @@
         steps(i * REST, REST)
         return carry
 
-    lax.fori_loop(0, large, large_step, 0)
-    lax.fori_loop(large * (UNROLL // REST), rounds, small_step, 0)
-
-    live_weight = jnp.where(weight > 0.5 * LOWEST, jnp.abs(weight), 0.0)
-    bad = jnp.where(jnp.max(live_weight) <= 128.0, 0.0, 1.0)
+    lax.fori_loop(0, large_steps, large_step, 0)
+    lax.fori_loop(large_steps * (UNROLL // REST), rounds, small_step, 0)
+
+    large = jnp.where((weight > 0.5 * LOWEST) & ~(jnp.abs(weight) <= 128.0), 1.0, 0.0)
+    bad = jnp.max(large, axis=0, keepdims=True)
+    bad = jnp.maximum(bad[:, 0:HALF], bad[:, HALF:])
     for half in range(2):
         cut = slice(half * HALF, (half + 1) * HALF)
         total = jnp.sum(r_ref[0:kept_blocks, half], axis=1)
         live = live_ref[:, cut] > 0.5 * LOWEST
         fine = (total >= 2.0**-86) & (total <= 2.0**126)
-        bad = bad + jnp.max(jnp.where(live, jnp.where(fine, 0.0, 1.0), 0.0))
+        off = jnp.where(live & ~fine, 1.0, 0.0)
+        bad = jnp.maximum(bad, jnp.max(off, axis=0, keepdims=True))
         out_ref[:, cut] = jnp.where(live, jnp.log2(jnp.where(live, total, 1.0)), LOWEST)
+    bad = jnp.max(bad)
 
     @pl.when(bad > 0.0)
     def _():
@@ -447,9 +483,7 @@
     positions = jnp.arange(BLOCK, dtype=jnp.int32)
 
     own_live = positions < courier_count[0]
-    tail = jnp.where(own_live, courier_cap, 0).reshape(4, EMB)
-    block = jnp.concatenate([courier_embed, jnp.pad(tail, ((0, 12), (0, 0)))], axis=0)
-    row = gather_row(block)
+    row = gather_row(*pack(courier_count, courier_embed, courier_cap))
     row, bias_in, adjacency, order_count = lax.optimization_barrier((row, bias_in, adjacency, order_count))
     orders = embed_orders(order_features, w_in, bias_in, w_out, bias_out)
     order_live = positions[None, :] < order_count[:, None]
@@ -459,15 +493,13 @@
 
     own = [row] + [plane_step(row, 1, step) for step in (1, 2, 3)]
     other = [other_core(row)] + [None] * 3
-    for step in (3, 2):
-        own[step], orders = lax.optimization_barrier((own[step], orders))
-        other[step] = other_core(own[step])
     parts = own + other
     (early_partial,) = first_half_sweep(
         True, early_list, early_rounds, zone, has, [parts[p] for p in EARLY], orders, live, "orders_1_early"
     )
-    own[1], early_partial = lax.optimization_barrier((own[1], early_partial))
-    other[1] = other_core(own[1])
+    own[1], own[2], own[3], early_partial = lax.optimization_barrier((own[1], own[2], own[3], early_partial))
+    for step in (1, 2, 3):
+        other[step] = other_core(own[step])
     late_partial, couriers, log_cap = first_half_sweep(
         False, late_list, late_rounds, zone, has, own + other, orders, live, "orders_1"
     )

time: 234 us -> 220 us (0.940); the launches traced: 232 us -> 221 us
  starting transfers between devices: 91.1 us -> 49.6 us
  Pallas kernels: 106 us -> 138 us
    pallas_call x3, Pallas kernels: 63.2 us -> 86.8 us  [half_sweep(): pl.pallas_call(kernel, out_shape=jax.ShapeDtypeStruct((kept_blocks, BLOCK...]
    ppermute x6, starting transfers between devices: 27 us -> 4.83 us  [along_z(): lax.ppermute(value, 'sub', [(i, (i + step) % SUBS) for i in range(SUBS)])]
    all_to_all x1, starting transfers between devices: 25.7 us -> 14.3 us  [shards(): parts = lax.all_to_all(partial, 'zone', 0, 0, tiled=True)]
    ppermute x12, starting transfers between devices: 30.1 us -> 20.1 us  [plane_step(): return lax.ppermute(value, 'zone', pairs)]
    pallas_call x2, Pallas kernels: 31.6 us -> 38.6 us  [first_half_sweep(): pl.pallas_call(kernel, out_shape=(jax.ShapeDtypeStruct((OB_DEV, BLOCK), j...]
  transfers between devices with their start and end apart: 24 -> 24, of which waited for: 16 -> 16; matrix products, arithmetic and copies ran while one was open for 1% -> 1% of each run, Pallas kernels for 11% -> 10%
where the time goes in v3:
time: 220 us; the launch traced here: 221 us
  Pallas kernels  138 us (63%)
  starting transfers between devices  49.6 us (23%)
  waiting for transfers between devices  26.5 us (12%)
  local copies, waits for them, and re-layouts  3.08 us (1%)
  other arithmetic  2.25 us (1%)
    pallas_call x3, Pallas kernels, half_sweep(): pl.pallas_call(kernel, out_shape=jax.ShapeDtypeStruct((kept_blocks, BLOCK...  86.8 us
    pallas_call x2, Pallas kernels, first_half_sweep(): pl.pallas_call(kernel, out_shape=(jax.ShapeDtypeStruct((OB_DEV, BLOCK), j...  38.6 us
    ppermute x12, starting transfers between devices, plane_step(): return lax.ppermute(value, 'zone', pairs)  20.1 us
    all_to_all x1, starting transfers between devices, shards(): parts = lax.all_to_all(partial, 'zone', 0, 0, tiled=True)  14.3 us
    ppermute x12, waiting for transfers between devices, plane_step(): return lax.ppermute(value, 'zone', pairs)  11.7 us
    ppermute x5, starting transfers between devices, other_core(): lax.ppermute(value, 'zone', [(zone_of(y, x, c), zone_of(y, x, 1 - c)) for...  10.4 us
    all_to_all x1, waiting for transfers between devices, shards(): parts = lax.all_to_all(partial, 'zone', 0, 0, tiled=True)  6.7 us
    pallas_call x1, Pallas kernels, embed_orders(): pl.pallas_call(embed_kernel, out_shape=jax.ShapeDtypeStruct((rows, EMB),...  6.63 us
  transfers between devices with their start and end apart: 24, of which 16 were waited for; matrix products, arithmetic and copies ran while one was open for 1% of the time, Pallas kernels for 10%

profile of v3, /device:TPU:1, one launch (start us, length us, event | category | flops | bytes accessed | tf_op | source)
XLA Modules:
  0.0 220.8 jit_solution(15718828290424496138)
XLA Ops:
  3.0 2.2 collective-permute-start
  5.2 2.6 %collective-permute-start.1 = (bf16[528,128]{1,0:T(8,128)(2,1)S(1)}, bf16[528,128]{1,0:T(8,128)(2,1)S(1)}, u32[]{:S(2)}, u32[]{:S(2)}) collective-permute-start(bf16[528,128]{1,0:T(8,128)(2,1)S(1)} %get-tuple-element.23), channel_id=1, source_target_pairs={{0,16},{4,68},{8,24},{12,76},{16,0},{20,84},{24,8},{28,92},{32,48}... | collective-permute-start | bytes 405512 | tf_op jit(solution)/shard_map/ppermute | solution.py:54
  9.3 2.6 %collective-permute-done.1 = bf16[528,128]{1,0:T(8,128)(2,1)S(1)} collective-permute-done((bf16[528,128]{1,0:T(8,128)(2,1)S(1)}, bf16[528,128]{1,0:T(8,128)(2,1)S(1)}, u32[]{:S(2)}, u32[]{:S(2)}) %collective-permute-start.1) | collective-permute-done | bytes 135200 | tf_op jit(solution)/shard_map/ppermute | solution.py:54
  12.0 1.9 collective-permute-start.6
  13.9 2.4 %collective-permute-start.5 = (bf16[2112,128]{1,0:T(8,128)(2,1)S(1)}, bf16[2112,128]{1,0:T(8,128)(2,1)S(1)}, u32[]{:S(2)}, u32[]{:S(2)}) collective-permute-start(bf16[2112,128]{1,0:T(8,128)(2,1)S(1)} %constant_dynamic-update-slice_fusion.refs_4_), channel_id=1, source_target_pairs={{0,96},{4,28},{8,104},{12,4},{16,112},{20,12},{24,120},{28,20},{32... | collective-permute-start | bytes 1622024 | tf_op jit(solution)/shard_map/ppermute | solution.py:54
  18.5 2.7 %first_lists.1 = (s32[272]{0:T(512)S(1)}, s32[272]{0:T(512)S(1)}, s32[1]{0:T(128)}, s32[1]{0:T(128)}, s32[32]{0:T(128)S(1)}) custom-call(s32[128]{0:T(128)S(1)} %get-tuple-element.46.pair_ref), custom_call_target="tpu_custom_call" | custom-call | tf_op jit(solution)/shard_map/first_lists/pallas_call | solution.py:241
  21.2 6.6 %embed_orders.1.refs_6_.refs_12_.refs_2_.refs_3_ = bf16[8192,128]{1,0:T(8,128)(2,1)S(1)} custom-call(bf16[8192,128]{1,0:T(8,128)(2,1)} %x_hbm.1, bf16[128,512]{1,0:T(8,128)(2,1)} %w_in_hbm.1, f32[1,512]{1,0:T(1,128)} %bitcast.19, bf16[512,128]{1,0:T(8,128)(2,1)} %w_out_hbm.1, f32[1,128]{1,0:T(1,128)} %bitcast.20), custom_call_target="tpu_custom_call" | custom-call | flops 2147483648 | bytes 4194304 | tf_op jit(solution)/shard_map/embed_orders/pallas_call | solution.py:175
  27.9 11.7 %orders_1_early.1 = f32[16,512]{1,0:T(8,128)S(1)} custom-call(s32[272]{0:T(512)S(1)} %get-tuple-element.30.refs_0_, s32[1]{0:T(128)} %get-tuple-element.31.refs_1_, s32[1]{0:T(128)} %bitcast.refs_2_, s32[32]{0:T(128)S(1)} %get-tuple-element.28.refs_3_, bf16[2112,128]{1,0:T(8,128)(2,1)S(1)} %constant_dynamic-update-slice_fusion.refs_4_, ...), custom_call_target="tpu_custom_call" | custom-call | flops 939524096 | bytes 6291456 | tf_op jit(solution)/shard_map/orders_1_early/pallas_call | solution.py:452
  39.7 4.4 %collective-permute-start.7 = (bf16[2112,128]{1,0:T(8,128)(2,1)S(1)}, bf16[2112,128]{1,0:T(8,128)(2,1)S(1)}, u32[]{:S(2)}, u32[]{:S(2)}) collective-permute-start(bf16[2112,128]{1,0:T(8,128)(2,1)S(1)} %collective-permute-done.3.refs_5_), channel_id=1, source_target_pairs={{0,4},{4,0},{8,12},{12,8},{16,20},{20,16},{24,28},{28,24},{32,36},... | collective-permute-start | bytes 1622024 | tf_op jit(solution)/shard_map/ppermute | solution.py:42
  47.2 26.9 %orders_1.1 = (f32[16,512]{1,0:T(8,128)S(1)}, bf16[16896,128]{1,0:T(8,128)(2,1)S(1)}, f32[32,512]{1,0:T(8,128)S(1)}) custom-call(s32[272]{0:T(512)S(1)} %get-tuple-element.26.refs_0_, s32[1]{0:T(128)} %get-tuple-element.27.refs_1_, s32[1]{0:T(128)} %bitcast.refs_2_, s32[32]{0:T(128)S(1)} %get-tuple-element.28.refs_3_, ...), custom_call_target="tpu_custom_call" | custom-call | flops 939524096 | bytes 6291456 | tf_op jit(solution)/shard_map/orders_1/pallas_call | solution.py:452
  74.1 2.5 %collective-permute-start.12 = (f32[16,512]{1,0:T(8,128)S(1)}, f32[16,512]{1,0:T(8,128)S(1)}, u32[]{:S(2)}, u32[]{:S(2)}) collective-permute-start(f32[16,512]{1,0:T(8,128)S(1)} %multiply_add_fusion.2), channel_id=1, source_target_pairs={{0,3},{1,0},{2,1},{3,2},{4,7},{5,4},{6,5},{7,6},{8,11},{9,8},{10,9... | collective-permute-start | bytes 98312 | tf_op jit(solution)/shard_map/ppermute | solution.py:46
  77.6 2.2 work_list.1
  81.0 29.0 %couriers_1.1 = f32[32,512]{1,0:T(8,128)S(1)} custom-call(s32[272]{0:T(512)S(1)} %get-tuple-element.37.refs_0_, s32[1]{0:T(128)} %get-tuple-element.38.refs_1_, bf16[8192,128]{1,0:T(8,128)(2,1)S(1)} %embed_orders.1.refs_6_.refs_12_.refs_2_.refs_3_, bf16[16896,128]{1,0:T(8,128)(2,1)S(1)} %get-tuple-element.39.refs_3_.refs_2_, ...), custom_call_target="tpu_custom_call" | custom-call | flops 1879048192 | bytes 6291456 | tf_op jit(solution)/shard_map/couriers_1/pallas_call | solution.py:385
  110.0 3.6 %collective-permute-start.13 = (f32[32,512]{1,0:T(8,128)S(1)}, f32[32,512]{1,0:T(8,128)S(1)}, u32[]{:S(2)}, u32[]{:S(2)}) collective-permute-start(f32[32,512]{1,0:T(8,128)S(1)} %couriers_1.1), channel_id=1, source_target_pairs={{0,4},{4,0},{8,12},{12,8},{16,20},{20,16},{24,28},{28,24},{32,36},... | collective-permute-start | bytes 196616 | tf_op jit(solution)/shard_map/ppermute | solution.py:42
  114.5 2.0 collective-permute-start.16
  116.5 7.2 %collective-permute-start.15 = (f32[32,512]{1,0:T(8,128)S(1)}, f32[32,512]{1,0:T(8,128)S(1)}, u32[]{:S(2)}, u32[]{:S(2)}) collective-permute-start(f32[32,512]{1,0:T(8,128)S(1)} %multiply_add_fusion.1), channel_id=1, source_target_pairs={{0,16},{4,68},{8,24},{12,76},{16,0},{20,84},{24,8},{28,92},{32,48}... | collective-permute-start | bytes 196616 | tf_op jit(solution)/shard_map/ppermute | solution.py:54
  123.7 1.6 collective-permute-done.15
  125.3 2.7 %collective-permute-done.14 = f32[32,512]{1,0:T(8,128)S(1)} collective-permute-done((f32[32,512]{1,0:T(8,128)S(1)}, f32[32,512]{1,0:T(8,128)S(1)}, u32[]{:S(2)}, u32[]{:S(2)}) %collective-permute-start.14) | collective-permute-done | bytes 65568 | tf_op jit(solution)/shard_map/ppermute | solution.py:54
  131.5 2.8 %collective-permute-done.18 = f32[32,512]{1,0:T(8,128)S(1)} collective-permute-done((f32[32,512]{1,0:T(8,128)S(1)}, f32[32,512]{1,0:T(8,128)S(1)}, u32[]{:S(2)}, u32[]{:S(2)}) %collective-permute-start.18) | collective-permute-done | bytes 65568 | tf_op jit(solution)/shard_map/ppermute | solution.py:54
  134.7 28.8 %orders_2.1 = f32[16,512]{1,0:T(8,128)S(1)} custom-call(s32[272]{0:T(512)S(1)} %get-tuple-element.37.refs_0_, s32[1]{0:T(128)} %get-tuple-element.38.refs_1_, bf16[16896,128]{1,0:T(8,128)(2,1)S(1)} %get-tuple-element.39.refs_3_.refs_2_, bf16[8192,128]{1,0:T(8,128)(2,1)S(1)} %embed_orders.1.refs_6_.refs_12_.refs_2_.refs_3_, ...), custom_call_target="tpu_custom_call" | custom-call | flops 1879048192 | bytes 6291456 | tf_op jit(solution)/shard_map/orders_2/pallas_call | solution.py:385
  166.3 1.6 collective-permute-done.21
  168.8 29.0 %couriers_2.1 = f32[32,512]{1,0:T(8,128)S(1)} custom-call(s32[272]{0:T(512)S(1)} %get-tuple-element.37.refs_0_, s32[1]{0:T(128)} %get-tuple-element.38.refs_1_, bf16[8192,128]{1,0:T(8,128)(2,1)S(1)} %embed_orders.1.refs_6_.refs_12_.refs_2_.refs_3_, bf16[16896,128]{1,0:T(8,128)(2,1)S(1)} %get-tuple-element.39.refs_3_.refs_2_, ...), custom_call_target="tpu_custom_call" | custom-call | flops 1879048192 | bytes 6291456 | tf_op jit(solution)/shard_map/couriers_2/pallas_call | solution.py:385
  198.5 14.3 %all-to-all-start = ((f32[32,1,512]{2,1,0:T(1,128)}), f32[32,1,512]{2,1,0:T(1,128)S(1)}, u32[]{:S(2)}, u32[]{:S(2)}) async-start(f32[32,1,512]{2,1,0:T(1,128)} %copy.17), calls=%async_computation | async-start | bytes 131072 | tf_op jit(solution)/shard_map/all_to_all | solution.py:529
  213.4 6.7 %all-to-all-done = f32[32,1,512]{2,1,0:T(1,128)S(1)} async-done(((f32[32,1,512]{2,1,0:T(1,128)}), f32[32,1,512]{2,1,0:T(1,128)S(1)}, u32[]{:S(2)}, u32[]{:S(2)}) %all-to-all-start) | async-done | bytes 65568 | tf_op jit(solution)/shard_map/all_to_all | solution.py:529
  (67 shorter events, 21.5 us)
Async XLA Ops:
  3.0 6.3 %collective-permute-start = (bf16[528,128]{1,0:T(8,128)(2,1)S(1)}, bf16[528,128]{1,0:T(8,128)(2,1)S(1)}, u32[]{:S(2)}, u32[]{:S(2)}) collective-permute-start(bf16[528,128]{1,0:T(8,128)(2,1)S(1)} %get-tuple-element.23), channel_id=1, source_target_pairs={{0,8},{4,36},{8,16},{12,44},{16,24},{20,52},{24,0},{28,60},{32,40}... | collective-permute-start | bytes 405512 | tf_op jit(solution)/shard_map/ppermute | solution.py:54
  5.2 6.8 %collective-permute-start.1 = (bf16[528,128]{1,0:T(8,128)(2,1)S(1)}, bf16[528,128]{1,0:T(8,128)(2,1)S(1)}, u32[]{:S(2)}, u32[]{:S(2)}) collective-permute-start(bf16[528,128]{1,0:T(8,128)(2,1)S(1)} %get-tuple-element.23), channel_id=1, source_target_pairs={{0,16},{4,68},{8,24},{12,76},{16,0},{20,84},{24,8},{28,92},{32,48}... | collective-permute-start | bytes 405512 | tf_op jit(solution)/shard_map/ppermute | solution.py:54
  7.8 4.2 %collective-permute-start.2 = (bf16[528,128]{1,0:T(8,128)(2,1)S(1)}, bf16[528,128]{1,0:T(8,128)(2,1)S(1)}, u32[]{:S(2)}, u32[]{:S(2)}) collective-permute-start(bf16[528,128]{1,0:T(8,128)(2,1)S(1)} %get-tuple-element.23), channel_id=1, source_target_pairs={{0,24},{4,100},{8,0},{12,108},{16,8},{20,116},{24,16},{28,124},{32... | collective-permute-start | bytes 405512 | tf_op jit(solution)/shard_map/ppermute | solution.py:54
  12.0 15.9 %collective-permute-start.6 = (bf16[2112,128]{1,0:T(8,128)(2,1)S(1)}, bf16[2112,128]{1,0:T(8,128)(2,1)S(1)}, u32[]{:S(2)}, u32[]{:S(2)}) collective-permute-start(bf16[2112,128]{1,0:T(8,128)(2,1)S(1)} %constant_dynamic-update-slice_fusion.refs_4_), channel_id=1, source_target_pairs={{0,4},{4,0},{8,12},{12,8},{16,20},{20,16},{24,28},{28,24},{32,36},... | collective-permute-start | bytes 1622024 | tf_op jit(solution)/shard_map/ppermute | solution.py:42
  13.9 25.8 %collective-permute-start.5 = (bf16[2112,128]{1,0:T(8,128)(2,1)S(1)}, bf16[2112,128]{1,0:T(8,128)(2,1)S(1)}, u32[]{:S(2)}, u32[]{:S(2)}) collective-permute-start(bf16[2112,128]{1,0:T(8,128)(2,1)S(1)} %constant_dynamic-update-slice_fusion.refs_4_), channel_id=1, source_target_pairs={{0,96},{4,28},{8,104},{12,4},{16,112},{20,12},{24,120},{28,20},{32... | collective-permute-start | bytes 1622024 | tf_op jit(solution)/shard_map/ppermute | solution.py:54
  16.2 23.4 %collective-permute-start.4 = (bf16[2112,128]{1,0:T(8,128)(2,1)S(1)}, bf16[2112,128]{1,0:T(8,128)(2,1)S(1)}, u32[]{:S(2)}, u32[]{:S(2)}) collective-permute-start(bf16[2112,128]{1,0:T(8,128)(2,1)S(1)} %constant_dynamic-update-slice_fusion.refs_4_), channel_id=1, source_target_pairs={{0,64},{4,20},{8,72},{12,28},{16,80},{20,4},{24,88},{28,12},{32,96... | collective-permute-start | bytes 1622024 | tf_op jit(solution)/shard_map/ppermute | solution.py:54
  16.6 23.1 %collective-permute-start.3 = (bf16[2112,128]{1,0:T(8,128)(2,1)S(1)}, bf16[2112,128]{1,0:T(8,128)(2,1)S(1)}, u32[]{:S(2)}, u32[]{:S(2)}) collective-permute-start(bf16[2112,128]{1,0:T(8,128)(2,1)S(1)} %constant_dynamic-update-slice_fusion.refs_4_), channel_id=1, source_target_pairs={{0,32},{4,12},{8,40},{12,20},{16,48},{20,28},{24,56},{28,4},{32,64... | collective-permute-start | bytes 1622024 | tf_op jit(solution)/shard_map/ppermute | solution.py:54
  39.7 6.0 %collective-permute-start.7 = (bf16[2112,128]{1,0:T(8,128)(2,1)S(1)}, bf16[2112,128]{1,0:T(8,128)(2,1)S(1)}, u32[]{:S(2)}, u32[]{:S(2)}) collective-permute-start(bf16[2112,128]{1,0:T(8,128)(2,1)S(1)} %collective-permute-done.3.refs_5_), channel_id=1, source_target_pairs={{0,4},{4,0},{8,12},{12,8},{16,20},{20,16},{24,28},{28,24},{32,36},... | collective-permute-start | bytes 1622024 | tf_op jit(solution)/shard_map/ppermute | solution.py:42
  44.1 2.3 %collective-permute-start.8 = (bf16[2112,128]{1,0:T(8,128)(2,1)S(1)}, bf16[2112,128]{1,0:T(8,128)(2,1)S(1)}, u32[]{:S(2)}, u32[]{:S(2)}) collective-permute-start(bf16[2112,128]{1,0:T(8,128)(2,1)S(1)} %collective-permute-done.4.refs_6_), channel_id=1, source_target_pairs={{0,4},{4,0},{8,12},{12,8},{16,20},{20,16},{24,28},{28,24},{32,36},... | collective-permute-start | bytes 1622024 | tf_op jit(solution)/shard_map/ppermute | solution.py:42
  44.2 3.0 %collective-permute-start.9 = (bf16[2112,128]{1,0:T(8,128)(2,1)S(1)}, bf16[2112,128]{1,0:T(8,128)(2,1)S(1)}, u32[]{:S(2)}, u32[]{:S(2)}) collective-permute-start(bf16[2112,128]{1,0:T(8,128)(2,1)S(1)} %collective-permute-done.5.refs_7_), channel_id=1, source_target_pairs={{0,4},{4,0},{8,12},{12,8},{16,20},{20,16},{24,28},{28,24},{32,36},... | collective-permute-start | bytes 1622024 | tf_op jit(solution)/shard_map/ppermute | solution.py:42
  74.1 5.7 %collective-permute-start.12 = (f32[16,512]{1,0:T(8,128)S(1)}, f32[16,512]{1,0:T(8,128)S(1)}, u32[]{:S(2)}, u32[]{:S(2)}) collective-permute-start(f32[16,512]{1,0:T(8,128)S(1)} %multiply_add_fusion.2), channel_id=1, source_target_pairs={{0,3},{1,0},{2,1},{3,2},{4,7},{5,4},{6,5},{7,6},{8,11},{9,8},{10,9... | collective-permute-start | bytes 98312 | tf_op jit(solution)/shard_map/ppermute | solution.py:46
  76.6 4.3 %collective-permute-start.11 = (f32[16,512]{1,0:T(8,128)S(1)}, f32[16,512]{1,0:T(8,128)S(1)}, u32[]{:S(2)}, u32[]{:S(2)}) collective-permute-start(f32[16,512]{1,0:T(8,128)S(1)} %multiply_add_fusion.2), channel_id=1, source_target_pairs={{0,2},{1,3},{2,0},{3,1},{4,6},{5,7},{6,4},{7,5},{8,10},{9,11},{10,... | collective-permute-start | bytes 98312 | tf_op jit(solution)/shard_map/ppermute | solution.py:46
  76.6 4.3 %collective-permute-start.10 = (f32[16,512]{1,0:T(8,128)S(1)}, f32[16,512]{1,0:T(8,128)S(1)}, u32[]{:S(2)}, u32[]{:S(2)}) collective-permute-start(f32[16,512]{1,0:T(8,128)S(1)} %multiply_add_fusion.2), channel_id=1, source_target_pairs={{0,1},{1,2},{2,3},{3,0},{4,5},{5,6},{6,7},{7,4},{8,9},{9,10},{10,1... | collective-permute-start | bytes 98312 | tf_op jit(solution)/shard_map/ppermute | solution.py:46
  110.0 4.5 %collective-permute-start.13 = (f32[32,512]{1,0:T(8,128)S(1)}, f32[32,512]{1,0:T(8,128)S(1)}, u32[]{:S(2)}, u32[]{:S(2)}) collective-permute-start(f32[32,512]{1,0:T(8,128)S(1)} %couriers_1.1), channel_id=1, source_target_pairs={{0,4},{4,0},{8,12},{12,8},{16,20},{20,16},{24,28},{28,24},{32,36},... | collective-permute-start | bytes 196616 | tf_op jit(solution)/shard_map/ppermute | solution.py:42
  114.5 9.2 %collective-permute-start.16 = (f32[32,512]{1,0:T(8,128)S(1)}, f32[32,512]{1,0:T(8,128)S(1)}, u32[]{:S(2)}, u32[]{:S(2)}) collective-permute-start(f32[32,512]{1,0:T(8,128)S(1)} %multiply_add_fusion.1), channel_id=1, source_target_pairs={{0,24},{4,100},{8,0},{12,108},{16,8},{20,116},{24,16},{28,124},{32... | collective-permute-start | bytes 196616 | tf_op jit(solution)/shard_map/ppermute | solution.py:54
  116.5 8.8 %collective-permute-start.15 = (f32[32,512]{1,0:T(8,128)S(1)}, f32[32,512]{1,0:T(8,128)S(1)}, u32[]{:S(2)}, u32[]{:S(2)}) collective-permute-start(f32[32,512]{1,0:T(8,128)S(1)} %multiply_add_fusion.1), channel_id=1, source_target_pairs={{0,16},{4,68},{8,24},{12,76},{16,0},{20,84},{24,8},{28,92},{32,48}... | collective-permute-start | bytes 196616 | tf_op jit(solution)/shard_map/ppermute | solution.py:54
  123.7 4.3 %collective-permute-start.14 = (f32[32,512]{1,0:T(8,128)S(1)}, f32[32,512]{1,0:T(8,128)S(1)}, u32[]{:S(2)}, u32[]{:S(2)}) collective-permute-start(f32[32,512]{1,0:T(8,128)S(1)} %multiply_add_fusion.1), channel_id=1, source_target_pairs={{0,8},{4,36},{8,16},{12,44},{16,24},{20,52},{24,0},{28,60},{32,40}... | collective-permute-start | bytes 196616 | tf_op jit(solution)/shard_map/ppermute | solution.py:54
  128.1 3.4 %collective-permute-start.19 = (f32[32,512]{1,0:T(8,128)S(1)}, f32[32,512]{1,0:T(8,128)S(1)}, u32[]{:S(2)}, u32[]{:S(2)}) collective-permute-start(f32[32,512]{1,0:T(8,128)S(1)} %multiply_add_fusion), channel_id=1, source_target_pairs={{0,96},{4,28},{8,104},{12,4},{16,112},{20,12},{24,120},{28,20},{32... | collective-permute-start | bytes 196616 | tf_op jit(solution)/shard_map/ppermute | solution.py:54
  129.6 4.7 %collective-permute-start.18 = (f32[32,512]{1,0:T(8,128)S(1)}, f32[32,512]{1,0:T(8,128)S(1)}, u32[]{:S(2)}, u32[]{:S(2)}) collective-permute-start(f32[32,512]{1,0:T(8,128)S(1)} %multiply_add_fusion), channel_id=1, source_target_pairs={{0,64},{4,20},{8,72},{12,28},{16,80},{20,4},{24,88},{28,12},{32,96... | collective-permute-start | bytes 196616 | tf_op jit(solution)/shard_map/ppermute | solution.py:54
  129.6 5.0 %collective-permute-start.17 = (f32[32,512]{1,0:T(8,128)S(1)}, f32[32,512]{1,0:T(8,128)S(1)}, u32[]{:S(2)}, u32[]{:S(2)}) collective-permute-start(f32[32,512]{1,0:T(8,128)S(1)} %multiply_add_fusion), channel_id=1, source_target_pairs={{0,32},{4,12},{8,40},{12,20},{16,48},{20,28},{24,56},{28,4},{32,64... | collective-permute-start | bytes 196616 | tf_op jit(solution)/shard_map/ppermute | solution.py:54
  163.5 2.8 %collective-permute-start.22 = (f32[16,512]{1,0:T(8,128)S(1)}, f32[16,512]{1,0:T(8,128)S(1)}, u32[]{:S(2)}, u32[]{:S(2)}) collective-permute-start(f32[16,512]{1,0:T(8,128)S(1)} %orders_2.1), channel_id=1, source_target_pairs={{0,3},{1,0},{2,1},{3,2},{4,7},{5,4},{6,5},{7,6},{8,11},{9,8},{10,9... | collective-permute-start | bytes 98312 | tf_op jit(solution)/shard_map/ppermute | solution.py:46
  163.5 4.3 %collective-permute-start.21 = (f32[16,512]{1,0:T(8,128)S(1)}, f32[16,512]{1,0:T(8,128)S(1)}, u32[]{:S(2)}, u32[]{:S(2)}) collective-permute-start(f32[16,512]{1,0:T(8,128)S(1)} %orders_2.1), channel_id=1, source_target_pairs={{0,2},{1,3},{2,0},{3,1},{4,6},{5,7},{6,4},{7,5},{8,10},{9,11},{10,... | collective-permute-start | bytes 98312 | tf_op jit(solution)/shard_map/ppermute | solution.py:46
  164.1 4.6 %collective-permute-start.20 = (f32[16,512]{1,0:T(8,128)S(1)}, f32[16,512]{1,0:T(8,128)S(1)}, u32[]{:S(2)}, u32[]{:S(2)}) collective-permute-start(f32[16,512]{1,0:T(8,128)S(1)} %orders_2.1), channel_id=1, source_target_pairs={{0,1},{1,2},{2,3},{3,0},{4,5},{5,6},{6,7},{7,4},{8,9},{9,10},{10,1... | collective-permute-start | bytes 98312 | tf_op jit(solution)/shard_map/ppermute | solution.py:46
  198.5 21.6 %all-to-all-start = ((f32[32,1,512]{2,1,0:T(1,128)}), f32[32,1,512]{2,1,0:T(1,128)S(1)}, u32[]{:S(2)}, u32[]{:S(2)}) async-start(f32[32,1,512]{2,1,0:T(1,128)} %copy.17), calls=%async_computation | async-start | bytes 131072 | tf_op jit(solution)/shard_map/all_to_all | solution.py:529
  (3 other events, 74.8 us)
